TPU v7x, 32 devices: a whole 2x2x4 slice. The times are simulated.
32 devices in a mesh: crop: 2 (over y), rows: 4 (over x, core), hid: 4 (over z).
Axes of the slice: x: 2, y: 2, z: 4, core: 2. Of those that a mesh axis runs over, the one named last changes fastest.
Arguments:
- tokens: bfloat16 [2, 8, 64, 4096], P('crop', 'rows', None, 'hid'), may hold values from -6 to 6
- cotangent: bfloat16 [2, 8, 64, 4096], P('crop', 'rows', None, 'hid'), may hold values from -6 to 6
- weight_in: bfloat16 [256, 64, 5, 256], P('rows', 'hid'), may hold values from -0.15625 to 0.15625
- weight_out: bfloat16 [256, 64, 5, 256], P('rows', 'hid'), may hold values from -0.078125 to 0.078125
- mix_kernel: float32 [9, 16384], P(None, 'hid'), may hold values from -4 to 4
- block_rows: int32 [64, 5], P('hid'), may hold values from 0 to 15, as said below
Outputs:
- grad_tokens: bfloat16 [2, 8, 64, 4096], P('crop', 'rows', None, 'hid')
- grad_w_in: float32 [256, 64, 5, 256], P(('crop', 'rows'), 'hid')
- grad_w_out: float32 [256, 64, 5, 256], P(('crop', 'rows'), 'hid')
- grad_kernel: float32 [9, 16384], P(None, 'hid')
Inputs may be any that keep to these rules, and one draw needn't show every extreme that they name: In each block column c, block_rows[c, 0] is a label L and block_rows[c, k] for k >= 1 is L with bit k - 1 flipped, so the 5 entries of a column differ; every value is the label of equally many block columns.
All inputs are finite; a program needn't handle non-finite values.
Results may differ from a plain program's by a relative error of at most 0.019.
Values may be sent and summed in bfloat16 or wider, within the bound.
A program may use at most 128 MiB of HBM per device.

v0:
```python
import jax
import jax.numpy as jnp
from jax import lax
from jax.sharding import PartitionSpec as P

root_two_pi = 0.7978845608
cubic_coef = 0.044715
loss_scale = 0.03125


def padded(shard, sides, width):
    for axis, dim in sides:
        devices, length = (lax.axis_size(axis), shard.shape[dim])
        up = [(i, (i + 1) % devices) for i in range(devices - 1)]
        down = [(j, i) for i, j in up]
        last = lax.slice_in_dim(shard, length - width, length, axis=dim)
        initial = lax.slice_in_dim(shard, 0, width, axis=dim)
        before = lax.ppermute(last, axis, up)
        after = lax.ppermute(initial, axis, down)
        shard = jnp.concatenate([before, shard, after], axis=dim)
    return shard


def gelu_pair(preact):
    inner = root_two_pi * (preact + cubic_coef * preact * preact * preact)
    tanh_val = jnp.tanh(inner)
    gelu_out = 0.5 * preact * (1.0 + tanh_val)
    slopes = 0.5 * (1.0 + tanh_val) + 0.5 * preact * (1.0 - tanh_val * tanh_val) * root_two_pi * (
        1.0 + 3.0 * cubic_coef * preact * preact
    )
    return (gelu_out, slopes)


def on_device(tokens, cotangent, weight_in, weight_out, mix_kernel, block_rows):
    in_panel, out_panel = (
        lax.all_gather(weight_in, "rows", axis=0, tiled=True),
        lax.all_gather(weight_out, "rows", axis=0, tiled=True),
    )
    tok_full, cot_full = (
        lax.all_gather(tokens, "hid", axis=3, tiled=True),
        lax.all_gather(cotangent, "hid", axis=3, tiled=True),
    )
    crop_count, height, grid_width, depth_all = tok_full.shape
    tok_count = crop_count * height * grid_width
    block_size = in_panel.shape[0]
    col_count = in_panel.shape[1]
    nnz_count = in_panel.shape[2]
    block_count = depth_all // block_size
    hidden_local = col_count * block_size
    flat_rows = block_rows.reshape(-1)
    in_select = jnp.take(
        tok_full.reshape(tok_count, block_count, block_size), flat_rows, axis=1
    ).reshape(tok_count, col_count, nnz_count, block_size)
    grad_select = jnp.take(
        cot_full.reshape(tok_count, block_count, block_size), flat_rows, axis=1
    ).reshape(tok_count, col_count, nnz_count, block_size)
    pre_act = jnp.einsum("tckb,bcke->tce", in_select, in_panel, preferred_element_type=jnp.float32)
    gelu_out, slopes = gelu_pair(pre_act)
    active = gelu_out.astype(jnp.bfloat16).reshape(crop_count, height, grid_width, hidden_local)
    act_rim = padded(active, (("rows", 1),), 1)
    mix_grad = (
        jnp.einsum("tckd,fckd->tcf", grad_select, out_panel, preferred_element_type=jnp.float32)
        .astype(jnp.bfloat16)
        .reshape(crop_count, height, grid_width, hidden_local)
    )
    grad_rim = padded(mix_grad, (("rows", 1),), 1)
    act_pad = jnp.pad(act_rim.astype(jnp.float32), ((0, 0), (0, 0), (1, 1), (0, 0)))
    grad_pad = jnp.pad(grad_rim.astype(jnp.float32), ((0, 0), (0, 0), (1, 1), (0, 0)))
    grad_grid = mix_grad.astype(jnp.float32)
    mix_sum = jnp.zeros((crop_count, height, grid_width, hidden_local), jnp.float32)
    act_grad = jnp.zeros((crop_count, height, grid_width, hidden_local), jnp.float32)
    kern_terms = []
    for row_off in range(3):
        for col_off in range(3):
            tap = mix_kernel[3 * row_off + col_off]
            shifted = act_pad[:, row_off : row_off + height, col_off : col_off + grid_width]
            mix_sum = mix_sum + tap * shifted
            act_grad = (
                act_grad
                + tap
                * grad_pad[
                    :, 2 - row_off : 2 - row_off + height, 2 - col_off : 2 - col_off + grid_width
                ]
            )
            kern_terms.append(jnp.sum(shifted * grad_grid, axis=(0, 1, 2)))
    kern_local = jnp.stack(kern_terms, axis=0) * loss_scale
    mix_out = mix_sum.astype(jnp.bfloat16).reshape(tok_count, col_count, block_size)
    pre_grad = (act_grad.reshape(tok_count, col_count, block_size) * slopes).astype(jnp.bfloat16)
    kern_total = lax.psum(kern_local.astype(jnp.bfloat16), ("crop", "rows")).astype(jnp.float32)
    back_select = jnp.einsum(
        "tce,bcke->tckb", pre_grad, in_panel, preferred_element_type=jnp.float32
    )
    one_hot = (
        block_rows[:, :, None] == jnp.arange(block_count, dtype=jnp.int32)[None, None, :]
    ).astype(jnp.float32)
    token_terms = jnp.einsum(
        "tckb,ckr->trb", back_select, one_hot, precision=lax.Precision.HIGHEST
    ).reshape(crop_count, height, grid_width, depth_all)
    grad_tokens = lax.psum_scatter(
        token_terms.astype(jnp.bfloat16), "hid", scatter_dimension=3, tiled=True
    )
    first_term = jnp.einsum(
        "tckb,tce->bcke", in_select, pre_grad, preferred_element_type=jnp.float32
    )
    second_term = jnp.einsum(
        "tcf,tckd->fckd", mix_out, grad_select, preferred_element_type=jnp.float32
    )
    share_sums = lax.psum_scatter(
        (jnp.stack([first_term, second_term], axis=1) * loss_scale).astype(jnp.bfloat16),
        ("crop", "rows"),
        scatter_dimension=0,
        tiled=True,
    ).astype(jnp.float32)
    return (grad_tokens, share_sums[:, 0], share_sums[:, 1], kern_total)


def solution(mesh):
    placed = (
        P("crop", "rows", None, "hid"),
        P("crop", "rows", None, "hid"),
        P("rows", "hid", None, None),
        P("rows", "hid", None, None),
        P(None, "hid"),
        P("hid", None),
    )
    return jax.shard_map(
        on_device,
        mesh=mesh,
        in_specs=placed,
        out_specs=(
            P("crop", "rows", None, "hid"),
            P(("crop", "rows"), "hid", None, None),
            P(("crop", "rows"), "hid", None, None),
            P(None, "hid"),
        ),
        check_vma=False,
    )
```

profile of v0, /device:TPU:0, one launch (start us, length us, event | category | flops | bytes accessed | tf_op | source)
XLA Modules:
  0.0 492.9 jit_solution(12108084531151369509)
XLA Ops:
  8.7 4.1 copy.46
  12.9 1.7 copy-done
  14.6 2.4 copy.49
  17.9 22.4 %all-gather.9.cloned.1.call-done = bf16[1,2,64,4096]{3,2,1,0:T(8,128)(2,1)} async-done(((bf16[1,2,64,1024]{3,2,1,0:T(8,128)(2,1)}), bf16[1,2,64,4096]{3,2,1,0:T(8,128)(2,1)}) %all-gather.9.cloned.1.call-update) | async-done | bytes 1048592 | tf_op jit(solution)/shard_map/all_gather | solution.py:40
  42.1 27.2 %all-gather.5.cloned.1.call-done = bf16[1,2,64,4096]{3,2,1,0:T(8,128)(2,1)} async-done(((bf16[1,2,64,1024]{3,2,1,0:T(8,128)(2,1)}), bf16[1,2,64,4096]{3,2,1,0:T(8,128)(2,1)}) %all-gather.5.cloned.1.call-update) | async-done | bytes 1048592 | tf_op jit(solution)/shard_map/all_gather | solution.py:41
  71.1 5.7 %gather_fusion.1 = bf16[80,128,256]{2,1,0:T(8,128)(2,1)} fusion(bf16[128,16,256]{2,0,1:T(8,128)(2,1)S(1)} %copy.48, s32[1024]{0:T(1024)S(1)} %pad_clamp_fusion), kind=kCustom, calls=%fused_computation.1.clone | custom fusion | bytes 10486080 | tf_op jit(solution)/shard_map/jit(_take)/gather | solution.py:51
  76.8 6.1 %gather_fusion = bf16[80,128,256]{2,1,0:T(8,128)(2,1)} fusion(bf16[128,16,256]{2,0,1:T(8,128)(2,1)S(1)} %copy.45, s32[1024]{0:T(1024)S(1)} %pad_clamp_fusion), kind=kCustom, calls=%fused_computation.clone | custom fusion | bytes 10486080 | tf_op jit(solution)/shard_map/jit(_take)/gather | solution.py:54
  82.9 10.0 %broadcast_select_fusion.1 = (bf16[80,128,256]{2,1,0:T(8,128)(2,1)}, bf16[80,128,256]{2,1,0:T(8,128)(2,1)}) fusion(bf16[80,128,256]{2,1,0:T(8,128)(2,1)} %gather_fusion, pred[80]{0:T(512)(128)(4,1)S(1)} %compare_and_fusion, bf16[80,128,256]{2,1,0:T(8,128)(2,1)} %gather_fusion.1), kind=kLoop, calls=%fused_computation.18 | loop fusion | flops 5242880 | bytes 20971600 | tf_op jit(solution)/shard_map/jit(_take)/select_n | solution.py:54
  92.9 48.1 %all-gather.7.cloned.1.call-done = bf16[256,16,5,256]{3,0,2,1:T(8,128)(2,1)} async-done(((bf16[64,16,5,256]{3,0,2,1:T(8,128)(2,1)}), bf16[256,16,5,256]{3,0,2,1:T(8,128)(2,1)}) %all-gather.7.cloned.1.call-update) | async-done | bytes 10485776 | tf_op jit(solution)/shard_map/all_gather | solution.py:37
  141.0 9.1 %fusion.35 = bf16[128,16,256]{2,0,1:T(8,128)(2,1)S(1)} fusion(bf16[128,16,5,256]{3,0,2,1:T(8,128)(2,1)} %bitcast.105, bf16[256,16,5,256]{3,0,2,1:T(8,128)(2,1)} %all-gather.7.cloned.1.call-done), kind=kOutput, calls=%fused_computation.76 | convolution fusion | flops 1342701568 | bytes 16777216 | tf_op jit(solution)/shard_map/tckd,fckd->tcf/dot_general | solution.py:62
  151.3 2.2 collective-permute-start
  155.3 2.7 collective-permute-done.1
  158.4 2.1 fusion.18
  160.5 2.0 copy.69
  162.4 56.4 %all-gather.11.cloned.1.call-done = bf16[256,16,5,256]{3,0,2,1:T(8,128)(2,1)} async-done(((bf16[64,16,5,256]{3,0,2,1:T(8,128)(2,1)}), bf16[256,16,5,256]{3,0,2,1:T(8,128)(2,1)}) %all-gather.11.cloned.1.call-update) | async-done | bytes 10485776 | tf_op jit(solution)/shard_map/all_gather | solution.py:36
  218.8 9.4 %multiply_convert_fusion = (bf16[128,16,256]{2,0,1:T(8,128)(2,1)S(1)}, bf16[128,16,256]{2,0,1:T(8,128)(2,1)S(1)}) fusion(f32[128,16,256]{2,1,0:T(8,128)} %bitcast.114, bf16[128,16,5,256]{3,0,2,1:T(8,128)(2,1)} %bitcast.107, bf16[256,16,5,256]{3,0,2,1:T(8,128)(2,1)} %all-gather.11.cloned.1.call-done), kind=kOutput, calls=%fused_computation.75 | convolution fusion | flops 1353187328 | bytes 19922944 | tf_op jit(solution)/shard_map/tckb,bcke->tce/dot_general | solution.py:57
  228.2 1.6 copy.53
  231.5 2.2 collective-permute-start.2
  235.0 11.1 %convolution_bitcast_fusion.1 = f32[256,1,16,5,256]{0,4,3,2,1:T(8,128)} fusion(bf16[128,16,5,256]{3,0,2,1:T(8,128)(2,1)} %bitcast.108, bf16[128,16,256]{2,0,1:T(8,128)(2,1)S(1)} %get-tuple-element.29), kind=kOutput, calls=%fused_computation.7 | convolution fusion | flops 1342177280 | bytes 27262976 | tf_op jit(solution)/shard_map/tckb,tce->bcke/dot_general | solution.py:102
  246.4 2.5 fusion.32
  248.9 2.1 add_convert_fusion
  252.3 12.4 %convolution_bitcast_fusion = f32[256,1,16,5,256]{0,4,3,2,1:T(8,128)} fusion(bf16[128,16,5,256]{3,0,2,1:T(8,128)(2,1)} %bitcast.106, bf16[128,16,256,1]{2,1,0,3:T(8,128)(2,1)S(1)} %bitcast.113), kind=kOutput, calls=%fused_computation.6 | convolution fusion | flops 1342177280 | bytes 27262976 | tf_op jit(solution)/shard_map/tcf,tckd->fckd/dot_general | solution.py:105
  264.7 22.8 %fusion = bf16[256,2,16,5,256]{0,4,3,2,1:T(8,128)(2,1)} fusion(f32[256,1,16,5,256]{0,4,3,2,1:T(8,128)} %convolution_bitcast_fusion, f32[256,1,16,5,256]{0,4,3,2,1:T(8,128)} %convolution_bitcast_fusion.1), kind=kLoop, calls=%fused_computation.3 | loop fusion | flops 31457280 | bytes 62914560 | tf_op jit(solution)/shard_map/convert_element_type | solution.py:109
  287.4 29.6 %copy.56 = bf16[256,2,16,5,256]{4,2,3,1,0:T(8,128)(2,1)} copy(bf16[256,2,16,5,256]{0,4,3,2,1:T(8,128)(2,1)} %fusion) | data formatting | bytes 41943040 | tf_op jit(solution)/shard_map/convert_element_type | solution.py:109
  317.0 8.8 %reduce-scatter.3.cloned.1.call-start = ((), (), s32[]{:S(2)}) async-start(), calls=%async_computation.6 | async-start | bytes 1310720 | tf_op jit(solution)/shard_map/reduce_scatter | solution.py:99
  325.8 9.3 %convolution_bitcast_fusion.2 = f32[128,16,5,256]{3,0,2,1:T(8,128)S(1)} fusion(bf16[256,16,5,256]{3,0,2,1:T(8,128)(2,1)} %all-gather.11.cloned.1.call-done, bf16[128,16,256]{2,0,1:T(8,128)(2,1)S(1)} %get-tuple-element.29), kind=kOutput, calls=%fused_computation.31 | convolution fusion | flops 1342177280 | bytes 22020096 | tf_op jit(solution)/shard_map/tce,bcke->tckb/dot_general | solution.py:90
  335.1 11.1 %fusion.36 = bf16[128,16,256]{2,1,0:T(8,128)(2,1)S(1)} fusion(f32[128,16,5,256]{3,0,2,1:T(8,128)S(1)} %convolution_bitcast_fusion.2, s32[16,5]{0,1:T(8,128)S(1)} %copy-done.2), kind=kOutput, calls=%fused_computation.77 | convolution fusion | flops 503842048 | bytes 11534656 | tf_op jit(solution)/shard_map/tckb,ckr->trb/dot_general | solution.py:96
  347.6 1.6 convert_element_type.95
  349.3 106.4 %reduce-scatter.5.cloned.1.call-done = bf16[32,2,16,5,256]{4,2,3,1,0:T(8,128)(2,1)} async-done(((bf16[256,2,16,5,256]{4,2,3,1,0:T(8,128)(2,1)}), bf16[32,2,16,5,256]{4,2,3,1,0:T(8,128)(2,1)}) %reduce-scatter.5.cloned.1.call-update) | async-done | bytes 2621456 | tf_op jit(solution)/shard_map/reduce_scatter | solution.py:108
  455.7 2.5 convert_element_type.92
  458.1 2.9 slice_bitcast_fusion
  461.1 24.8 %reduce-scatter.3.cloned.1.call-done = bf16[1,2,64,1024]{3,2,1,0:T(8,128)(2,1)} async-done(((bf16[1,2,64,4096]{3,2,1,0:T(8,128)(2,1)}), bf16[1,2,64,1024]{3,2,1,0:T(8,128)(2,1)}) %reduce-scatter.3.cloned.1.call-update) | async-done | bytes 262160 | tf_op jit(solution)/shard_map/reduce_scatter | solution.py:99
  (45 shorter events, 15.2 us)
Async XLA Ops:
  7.2 33.1 %all-gather.9.cloned.1.call-start = ((), (), s32[]{:S(2)}) async-start(), calls=%async_computation.4 | async-start | bytes 1310720 | tf_op jit(solution)/shard_map/all_gather | solution.py:40
  7.9 61.4 %all-gather.5.cloned.1.call-start = ((), (), s32[]{:S(2)}) async-start(), calls=%async_computation.2 | async-start | bytes 1310720 | tf_op jit(solution)/shard_map/all_gather | solution.py:41
  8.6 132.4 %all-gather.7.cloned.1.call-start = ((), (), s32[]{:S(2)}) async-start(), calls=%async_computation.3 | async-start | bytes 13107200 | tf_op jit(solution)/shard_map/all_gather | solution.py:37
  12.8 1.7 copy-start
  12.9 206.0 %all-gather.11.cloned.1.call-start = ((), (), s32[]{:S(2)}) async-start(), calls=%async_computation.5 | async-start | bytes 13107200 | tf_op jit(solution)/shard_map/all_gather | solution.py:36
  17.0 0.7 copy-start.2
  17.0 330.6 %all-reduce.4.cloned.1.call-start = ((), (), s32[]{:S(2)}) async-start(), calls=%async_computation.8 | async-start | bytes 262144 | tf_op jit(solution)/shard_map/psum | solution.py:89
  150.7 4.4 copy-start.1
  151.3 4.0 collective-permute-start
  153.5 4.6 collective-permute-start.1
  231.5 14.6 %collective-permute-start.2 = (bf16[1,1,64,4096]{3,2,1,0:T(8,128)(2,1)S(1)}, bf16[1,1,64,4096]{3,2,1,0:T(8,128)(2,1)S(1)}, u32[]{:S(2)}, u32[]{:S(2)}) collective-permute-start(bf16[1,1,64,4096]{3,2,1,0:T(8,128)(2,1)S(1)} %get-tuple-element.30), channel_id=1, source_target_pairs={{0,4},{4,8},{8,12},{1,5},{5,9},{9,13},{2,6},{6,10},{10,14},{3,7},{... | collective-permute-start | bytes 1572872 | tf_op jit(solution)/shard_map/ppermute | solution.py:18
  233.7 12.4 %collective-permute-start.3 = (bf16[1,1,64,4096]{3,2,1,0:T(8,128)(2,1)S(1)}, bf16[1,1,64,4096]{3,2,1,0:T(8,128)(2,1)S(1)}, u32[]{:S(2)}, u32[]{:S(2)}) collective-permute-start(bf16[1,1,64,4096]{3,2,1,0:T(8,128)(2,1)S(1)} %get-tuple-element.31), channel_id=1, source_target_pairs={{4,0},{8,4},{12,8},{5,1},{9,5},{13,9},{6,2},{10,6},{14,10},{7,3},{... | collective-permute-start | bytes 1572872 | tf_op jit(solution)/shard_map/ppermute | solution.py:19
  252.2 203.5 %reduce-scatter.5.cloned.1.call-start = ((), (), s32[]{:S(2)}) async-start(), calls=%async_computation.7 | async-start | bytes 23592960 | tf_op jit(solution)/shard_map/reduce_scatter | solution.py:108
  317.0 168.8 %reduce-scatter.3.cloned.1.call-start = ((), (), s32[]{:S(2)}) async-start(), calls=%async_computation.6 | async-start | bytes 1310720 | tf_op jit(solution)/shard_map/reduce_scatter | solution.py:99
Sparse Core Ops, SparseCore 0:
  9.5 30.6 all-gather.8
  41.8 27.4 all-gather.4
  71.4 69.5 all-gather.6
  143.0 75.7 all-gather.10
  252.3 55.5 all-reduce.3
  317.2 138.4 reduce-scatter.4
  458.5 27.3 reduce-scatter.2
where the time goes:
time: 502 us; the launch traced here: 493 us
  waiting for transfers between devices  290 us (58%)
  local copies, waits for them, and re-layouts  65.1 us (13%)
  matrix products  62.4 us (12%)
  other arithmetic  44.9 us (9%)
  starting transfers between devices  16.2 us (3%)
  between operations  14.6 us (3%)
    reduce_scatter x1, waiting for transfers between devices, on_device(): lax.psum_scatter((jnp.stack([first_term, second_term], axis=1) * loss_sca...  106 us
    all_gather x1, waiting for transfers between devices, on_device(): lax.all_gather(weight_in, 'rows', axis=0, tiled=True)  56.4 us
    all_gather x1, waiting for transfers between devices, on_device(): lax.all_gather(weight_out, 'rows', axis=0, tiled=True)  48.1 us
    convert_element_type x1, local copies, waits for them, and re-layouts, on_device(): (jnp.stack([first_term, second_term], axis=1) * loss_scale).astype(jnp.bf...  29.6 us
    all_gather x1, waiting for transfers between devices, on_device(): lax.all_gather(cotangent, 'hid', axis=3, tiled=True)  27.2 us
    reduce_scatter x1, waiting for transfers between devices, on_device(): lax.psum_scatter(token_terms.astype(jnp.bfloat16), 'hid', scatter_dimensi...  24.8 us
    convert_element_type x1, other arithmetic, on_device(): (jnp.stack([first_term, second_term], axis=1) * loss_scale).astype(jnp.bf...  22.8 us
    all_gather x1, waiting for transfers between devices, on_device(): lax.all_gather(tokens, 'hid', axis=3, tiled=True)  22.4 us
  transfers between devices with their start and end apart: 11, of which 8 were waited for; matrix products, arithmetic and copies ran while one was open for 31% of the time, Pallas kernels for 0%

commit v1 on v0

--- a/solution.py
+++ b/solution.py
@@ -1,11 +1,462 @@
+import functools
+
 import jax
 import jax.numpy as jnp
 from jax import lax
+from jax.experimental import pallas as pl
+from jax.experimental.pallas import tpu as pltpu
 from jax.sharding import PartitionSpec as P
 
 root_two_pi = 0.7978845608
 cubic_coef = 0.044715
 loss_scale = 0.03125
+
+MESH_ID = pl.DeviceIdType.MESH
+ANY = pl.BlockSpec(memory_space=pl.ANY)
+VMEM = pl.BlockSpec(memory_space=pltpu.VMEM)
+SMEM = pl.BlockSpec(memory_space=pltpu.SMEM)
+
+
+def span(start, size):
+    return pl.ds(pl.multiple_of(start * size, size), size)
+
+
+def neighbours():
+    y, r, z = lax.axis_index("crop"), lax.axis_index("rows"), lax.axis_index("hid")
+    x, core = r // 2, r % 2
+    same_chip = x * 2 + (1 - core)
+    across = (1 - x) * 2 + core
+    diagonal = (1 - x) * 2 + (1 - core)
+    return y, r, z, same_chip, across, diagonal
+
+
+def enter(partners):
+    barrier = pltpu.get_barrier_semaphore()
+    for partner in partners:
+        pl.semaphore_signal(barrier, inc=1, device_id=partner, device_id_type=MESH_ID)
+    pl.semaphore_wait(barrier, len(partners))
+
+
+def remote(src, dst, send_sem, recv_sem, target):
+    return pltpu.make_async_remote_copy(
+        src_ref=src,
+        dst_ref=dst,
+        send_sem=send_sem,
+        recv_sem=recv_sem,
+        device_id=target,
+        device_id_type=MESH_ID,
+    )
+
+
+def gather_kernel(
+    depth, tok, cot, w_in, w_out, tok_all, cot_all, in_all, out_all,
+    tok_send, tok_recv, w_send, w_recv, own_sem,
+):
+    y, r, z, same_chip, across, diagonal = neighbours()
+    tokens, features = tok.shape
+    rows = w_in.shape[0]
+    lanes = in_all.shape[1]
+    half = rows // 2
+    enter(
+        [{"rows": same_chip}, {"rows": across}, {"rows": diagonal}, {"crop": 1 - y}]
+        + [{"hid": (z + step) % depth} for step in range(1, depth)]
+    )
+    streams = ((tok, tok_all), (cot, cot_all))
+    panels = ((w_in, in_all), (w_out, out_all))
+    started, local = [], []
+
+    def piece(full, row, col):
+        return full.at[span(row, tokens), span(col, features)]
+
+    def send_piece(a, src, row, col, slot, target):
+        copy = remote(
+            src, piece(streams[a][1], row, col), tok_send.at[a, slot], tok_recv.at[a, row, col], target
+        )
+        copy.start()
+        started.append(copy)
+
+    def await_piece(a, row, col):
+        part = piece(streams[a][1], row, col)
+        remote(
+            part, part, tok_send.at[a, 0], tok_recv.at[a, row, col], {"rows": same_chip}
+        ).wait_recv()
+        return part
+
+    def half_rows(full, row, h):
+        return full.at[pl.ds(pl.multiple_of(row * rows + h * half, half), half), :]
+
+    for a in range(2):
+        src = streams[a][0]
+        for step in range(1, depth):
+            send_piece(a, src, r, z, step - 1, {"hid": (z + step) % depth})
+        send_piece(a, src, r, z, depth - 1, {"rows": across})
+    for a in range(2):
+        src, full = panels[a]
+        for slot, dest in ((1, across), (2, diagonal)):
+            copy = remote(
+                src.at[span(y, half), span(dest, lanes)],
+                half_rows(full, r, y),
+                w_send.at[a, slot],
+                w_recv.at[a, r, y],
+                {"rows": dest},
+            )
+            copy.start()
+            started.append(copy)
+        copy = remote(
+            src.at[:, span(same_chip, lanes)],
+            full.at[span(r, rows), :],
+            w_send.at[a, 0],
+            w_recv.at[a, r, 0],
+            {"rows": same_chip},
+        )
+        copy.start()
+        started.append(copy)
+        send_piece(a, streams[a][0], r, z, depth, {"rows": same_chip})
+        local.append(pltpu.make_async_copy(streams[a][0], piece(streams[a][1], r, z), own_sem.at[a, 0]))
+        local.append(
+            pltpu.make_async_copy(
+                src.at[:, span(r, lanes)], full.at[span(r, rows), :], own_sem.at[a, 1]
+            )
+        )
+    for copy in local:
+        copy.start()
+    for step in range(1, depth):
+        col = (z + step) % depth
+        for a in range(2):
+            part = await_piece(a, r, col)
+            send_piece(a, part, r, col, depth + 2 * step - 1, {"rows": across})
+            send_piece(a, part, r, col, depth + 2 * step, {"rows": same_chip})
+    for a in range(2):
+        full = panels[a][1]
+        for slot, row in ((3, across), (4, diagonal)):
+            part = half_rows(full, row, y)
+            copy = remote(
+                part, part, w_send.at[a, slot], w_recv.at[a, row, y], {"rows": row}
+            )
+            copy.wait_recv()
+            copy = remote(
+                part, part, w_send.at[a, slot], w_recv.at[a, row, y], {"crop": 1 - y}
+            )
+            copy.start()
+            started.append(copy)
+    for step in range(depth):
+        col = (z + step) % depth
+        for a in range(2):
+            part = await_piece(a, across, col)
+            send_piece(a, part, across, col, 3 * depth - 1 + step, {"rows": same_chip})
+    for a in range(2):
+        full = panels[a][1]
+        part = full.at[span(same_chip, rows), :]
+        remote(
+            part, part, w_send.at[a, 0], w_recv.at[a, same_chip, 0], {"rows": same_chip}
+        ).wait_recv()
+        for row in (across, diagonal):
+            part = half_rows(full, row, 1 - y)
+            remote(
+                part, part, w_send.at[a, 0], w_recv.at[a, row, 1 - y], {"crop": 1 - y}
+            ).wait_recv()
+        for row in (same_chip, diagonal):
+            for step in range(depth):
+                await_piece(a, row, (z + step) % depth)
+    for copy in local:
+        copy.wait()
+    for copy in started:
+        copy.wait_send()
+
+
+def nt(a, b):
+    return lax.dot_general(a, b, (((1,), (1,)), ((), ())), preferred_element_type=jnp.float32)
+
+
+def tn(a, b):
+    return lax.dot_general(a, b, (((0,), (0,)), ((), ())), preferred_element_type=jnp.float32)
+
+
+def local_kernel(
+    width, block, cols, nnz, ids, tok, cot, w_in, w_out, taps,
+    dx_out, gw_in, gw_out, kern, dx, pre_s, act_s, slope_s, mg_s,
+):
+    count = tok.shape[0]
+    dx[...] = jnp.zeros_like(dx)
+    place = lax.broadcasted_iota(jnp.int32, (count, block), 0) % width
+    kern[...] = jnp.zeros_like(kern)
+
+    def spread(value):
+        before = jnp.where(place == 0, 0.0, pltpu.roll(value, 1, 0))
+        after = jnp.where(place == width - 1, 0.0, pltpu.roll(value, count - 1, 0))
+        return (before, value, after)
+
+    def stack_rows(up, mid, down):
+        edge = jnp.zeros((width, block), jnp.float32)
+        return (
+            mid
+            + jnp.concatenate([edge, up[:-width]], axis=0)
+            + jnp.concatenate([down[width:], edge], axis=0)
+        )
+
+    def column(c, carry):
+        hidden = span(c, block)
+
+        def feats(k):
+            return span(ids[c * nnz + k], block)
+
+        def panel(k):
+            return span(c * nnz + k, block)
+
+        pre = jnp.dot(tok[:, feats(0)], w_in[:, panel(0)], preferred_element_type=jnp.float32)
+        for k in range(1, nnz):
+            pre += jnp.dot(tok[:, feats(k)], w_in[:, panel(k)], preferred_element_type=jnp.float32)
+        pre_s[...] = pre
+        mg = nt(cot[:, feats(0)], w_out[:, panel(0)])
+        for k in range(1, nnz):
+            mg += nt(cot[:, feats(k)], w_out[:, panel(k)])
+        mg_s[...] = mg.astype(jnp.bfloat16).astype(jnp.float32)
+        p = pre_s[...]
+        t = jnp.tanh(root_two_pi * (p + cubic_coef * p * p * p))
+        act_s[...] = (0.5 * p * (1.0 + t)).astype(jnp.bfloat16).astype(jnp.float32)
+        slope_s[...] = 0.5 * (1.0 + t) + 0.5 * p * (1.0 - t * t) * root_two_pi * (
+            1.0 + 3.0 * cubic_coef * p * p
+        )
+
+        def tap(a, b):
+            row = 3 * (a + 1) + (b + 1)
+            return taps[row : row + 1, hidden]
+
+        acts = spread(act_s[...])
+        mixed = stack_rows(
+            *[sum(tap(a, b) * acts[b + 1] for b in (-1, 0, 1)) for a in (-1, 0, 1)]
+        ).astype(jnp.bfloat16)
+        grads = mg_s[...]
+        for b in (-1, 0, 1):
+            seen = acts[b + 1]
+            sums = (
+                jnp.sum(seen[:-width] * grads[width:], axis=0, keepdims=True),
+                jnp.sum(seen * grads, axis=0, keepdims=True),
+                jnp.sum(seen[width:] * grads[:-width], axis=0, keepdims=True),
+            )
+            for a in (-1, 0, 1):
+                row = 3 * (a + 1) + (b + 1)
+                kern[row : row + 1, hidden] = sums[a + 1] * loss_scale
+        for k in range(nnz):
+            gw_out[:, panel(k)] = (tn(mixed, cot[:, feats(k)]) * loss_scale).astype(jnp.bfloat16)
+        backs = spread(mg_s[...])
+        gathered = stack_rows(
+            *[sum(tap(a, b) * backs[1 - b] for b in (-1, 0, 1)) for a in (1, 0, -1)]
+        )
+        pre_grad = (gathered * slope_s[...]).astype(jnp.bfloat16)
+        for k in range(nnz):
+            gw_in[:, panel(k)] = (tn(tok[:, feats(k)], pre_grad) * loss_scale).astype(jnp.bfloat16)
+            dx[:, feats(k)] += nt(pre_grad, w_in[:, panel(k)])
+        return carry
+
+    lax.fori_loop(0, cols, column, 0)
+    dx_out[...] = dx[...].astype(jnp.bfloat16)
+
+
+def scatter_kernel(
+    depth, dx, gw_in, gw_out, kern, dx_mine, in_mine, out_mine, kern_all,
+    dx_near, dx_half, dx_far, dx_sum, dx_last, gw_part, gw_sum, kern_part,
+    dx_send, dx_recv, gw_send, gw_recv, kern_send, kern_recv,
+):
+    y, r, z, same_chip, across, diagonal = neighbours()
+    group = [same_chip, across, diagonal]
+    enter(
+        [{"rows": row} for row in group]
+        + [{"crop": 1 - y, "rows": row} for row in group]
+        + [{"crop": 1 - y}]
+        + [{"hid": (z + step) % depth} for step in range(1, depth)]
+    )
+    started = []
+
+    def go(*args):
+        copy = remote(*args)
+        copy.start()
+        started.append(copy)
+
+    tokens, features = dx_mine.shape
+    rows = in_mine.shape[0]
+    lanes = gw_in.shape[1]
+    weights = ((gw_in, in_mine), (gw_out, out_mine))
+    for slot, row in enumerate((diagonal, same_chip)):
+        go(dx.at[span(row, tokens), :], dx_near.at[slot], dx_send.at[slot], dx_recv.at[slot], {"rows": same_chip})
+    order = (across, diagonal, same_chip, r)
+    for slot, row in enumerate(order):
+        for a in range(2):
+            go(
+                weights[a][0].at[span((1 - y) * 4 + row, rows), :],
+                gw_part.at[a, slot],
+                gw_send.at[a, slot],
+                gw_recv.at[a, slot],
+                {"crop": 1 - y},
+            )
+    for slot, row in enumerate(group):
+        go(kern, kern_part.at[y, r], kern_send.at[slot], kern_recv.at[y, r], {"rows": row})
+        go(
+            kern,
+            kern_part.at[y, r],
+            kern_send.at[slot + 3],
+            kern_recv.at[y, r],
+            {"crop": 1 - y, "rows": row},
+        )
+    go(kern, kern_part.at[y, r], kern_send.at[6], kern_recv.at[y, r], {"crop": 1 - y})
+
+    def arrived(ref, send_sem, recv_sem, target):
+        remote(ref, ref, send_sem, recv_sem, target).wait_recv()
+
+    arrived(dx_near.at[0], dx_send.at[0], dx_recv.at[0], {"rows": same_chip})
+    dx_half[...] = (
+        dx[span(across, tokens), :].astype(jnp.float32) + dx_near[0].astype(jnp.float32)
+    ).astype(jnp.bfloat16)
+    go(dx_half, dx_far, dx_send.at[2], dx_recv.at[2], {"rows": across})
+    arrived(dx_near.at[1], dx_send.at[1], dx_recv.at[1], {"rows": same_chip})
+    arrived(dx_far, dx_send.at[2], dx_recv.at[2], {"rows": across})
+    for col in range(depth):
+        part = slice(col * features, (col + 1) * features)
+        dx_sum[col] = (
+            dx[span(r, tokens), part].astype(jnp.float32)
+            + dx_near[1, :, part].astype(jnp.float32)
+            + dx_far[:, part].astype(jnp.float32)
+        ).astype(jnp.bfloat16)
+    for step in range(1, depth):
+        go(
+            dx_sum.at[(z + step) % depth],
+            dx_last.at[step - 1],
+            dx_send.at[2 + step],
+            dx_recv.at[2 + step],
+            {"hid": (z + step) % depth},
+        )
+    for slot, row in enumerate(order):
+        for a in range(2):
+            arrived(gw_part.at[a, slot], gw_send.at[a, slot], gw_recv.at[a, slot], {"crop": 1 - y})
+            total = (
+                weights[a][0][span(y * 4 + row, rows), :].astype(jnp.float32)
+                + gw_part[a, slot].astype(jnp.float32)
+            ).astype(jnp.bfloat16)
+            if slot == 3:
+                weights[a][1][:, span(r, lanes)] = total
+            else:
+                gw_sum[a, slot] = total
+                go(
+                    gw_sum.at[a, slot],
+                    weights[a][1].at[:, span(r, lanes)],
+                    gw_send.at[a, 4 + slot],
+                    gw_recv.at[a, 4 + slot],
+                    {"rows": row},
+                )
+    total = dx_sum[z].astype(jnp.float32)
+    for step in range(1, depth):
+        arrived(dx_last.at[step - 1], dx_send.at[2 + step], dx_recv.at[2 + step], {"hid": (z + step) % depth})
+        total += dx_last[step - 1].astype(jnp.float32)
+    dx_mine[...] = total.astype(jnp.bfloat16)
+    kern_part[y, r] = kern[...]
+    for row in group:
+        for crop in (y, 1 - y):
+            arrived(kern_part.at[crop, row], kern_send.at[0], kern_recv.at[crop, row], {"rows": same_chip})
+    arrived(kern_part.at[1 - y, r], kern_send.at[0], kern_recv.at[1 - y, r], {"rows": same_chip})
+    wide = kern.shape[1]
+    for row in range(4):
+        kern_all[:, row * wide : (row + 1) * wide] = kern_part[0, row].astype(
+            jnp.float32
+        ) + kern_part[1, row].astype(jnp.float32)
+    for slot, row in enumerate(order[:3]):
+        for a in range(2):
+            arrived(
+                weights[a][1].at[:, span(row, lanes)],
+                gw_send.at[a, 4 + slot],
+                gw_recv.at[a, 4 + slot],
+                {"rows": row},
+            )
+    for copy in started:
+        copy.wait_send()
+
+
+def split_hidden(tokens, cotangent, weight_in, weight_out, mix_kernel, block_rows):
+    n_rows, depth = lax.axis_size("rows"), lax.axis_size("hid")
+    _, height, width, features = tokens.shape
+    rows, all_cols, nnz, block = weight_in.shape
+    count = height * width
+    whole = count * n_rows
+    model = features * depth
+    cols = all_cols // n_rows
+    lanes = cols * nnz * block
+    hidden = cols * block
+    bf16, f32 = jnp.bfloat16, jnp.float32
+    dma, sds = pltpu.SemaphoreType.DMA, jax.ShapeDtypeStruct
+    params = functools.partial(pltpu.CompilerParams, vmem_limit_bytes=60 * 1024 * 1024)
+    tok_all, cot_all, in_all, out_all = pl.pallas_call(
+        functools.partial(gather_kernel, depth),
+        name="gather_parts",
+        out_shape=[sds((whole, model), bf16)] * 2 + [sds((rows * n_rows, lanes), bf16)] * 2,
+        in_specs=[ANY] * 4,
+        out_specs=[ANY] * 4,
+        scratch_shapes=[
+            dma((2, 4 * depth)),
+            dma((2, n_rows, depth)),
+            dma((2, 5)),
+            dma((2, n_rows, 2)),
+            dma((2, 2)),
+        ],
+        compiler_params=pltpu.CompilerParams(collective_id=1, has_side_effects=True),
+    )(
+        tokens.reshape(count, features),
+        cotangent.reshape(count, features),
+        weight_in.reshape(rows, all_cols * nnz * block),
+        weight_out.reshape(rows, all_cols * nnz * block),
+    )
+    me = lax.axis_index("rows")
+    taps = lax.dynamic_slice_in_dim(mix_kernel, me * hidden, hidden, axis=1)
+    ids = lax.dynamic_slice_in_dim(block_rows, me * cols, cols, axis=0).reshape(-1)
+    dx, gw_in, gw_out, kern = pl.pallas_call(
+        functools.partial(local_kernel, width, block, cols, nnz),
+        name="local_math",
+        out_shape=[
+            sds((whole, model), bf16),
+            sds((block, lanes), bf16),
+            sds((block, lanes), bf16),
+            sds((16, hidden), f32),
+        ],
+        in_specs=[SMEM] + [VMEM] * 5,
+        out_specs=[VMEM] * 4,
+        scratch_shapes=[pltpu.VMEM((whole, model), f32)] + [pltpu.VMEM((whole, block), f32)] * 4,
+        compiler_params=params(),
+    )(ids, tok_all, cot_all, in_all, out_all, taps)
+    out_rows = block // (n_rows * lax.axis_size("crop"))
+    dx_mine, in_mine, out_mine, kern_all = pl.pallas_call(
+        functools.partial(scatter_kernel, depth),
+        name="scatter_sums",
+        out_shape=[
+            sds((count, features), bf16),
+            sds((out_rows, all_cols * nnz * block), bf16),
+            sds((out_rows, all_cols * nnz * block), bf16),
+            sds((16, hidden * n_rows), f32),
+        ],
+        in_specs=[VMEM] * 4,
+        out_specs=[VMEM] * 4,
+        scratch_shapes=[
+            pltpu.VMEM((2, count, model), bf16),
+            pltpu.VMEM((count, model), bf16),
+            pltpu.VMEM((count, model), bf16),
+            pltpu.VMEM((depth, count, features), bf16),
+            pltpu.VMEM((depth - 1, count, features), bf16),
+            pltpu.VMEM((2, 4, out_rows, lanes), bf16),
+            pltpu.VMEM((2, 3, out_rows, lanes), bf16),
+            pltpu.VMEM((2, n_rows, 16, hidden), bf16),
+            dma((2 + depth,)),
+            dma((2 + depth,)),
+            dma((2, 7)),
+            dma((2, 7)),
+            dma((7,)),
+            dma((2, n_rows)),
+        ],
+        compiler_params=params(collective_id=2, has_side_effects=True),
+    )(dx, gw_in, gw_out, kern.astype(bf16))
+    shape = (out_rows, all_cols, nnz, block)
+    return (
+        dx_mine.reshape(tokens.shape),
+        in_mine.astype(f32).reshape(shape),
+        out_mine.astype(f32).reshape(shape),
+        kern_all[: mix_kernel.shape[0]],
+    )
 
 
 def padded(shard, sides, width):
@@ -123,8 +574,22 @@
         P(None, "hid"),
         P("hid", None),
     )
+    n_crop, n_rows = mesh.shape["crop"], mesh.shape["rows"]
+    n_hid = mesh.shape["hid"]
+
+    def step(tokens, cotangent, weight_in, weight_out, mix_kernel, block_rows):
+        fits = (
+            n_crop == 2
+            and n_rows == 4
+            and tokens.shape[0] == 1
+            and weight_in.shape[1] % n_rows == 0
+            and tokens.shape[1] * tokens.shape[2] * n_rows * tokens.shape[3] * n_hid <= 2**22
+        )
+        chosen = split_hidden if fits else on_device
+        return chosen(tokens, cotangent, weight_in, weight_out, mix_kernel, block_rows)
+
     return jax.shard_map(
-        on_device,
+        step,
         mesh=mesh,
         in_specs=placed,
         out_specs=(

time: 502 us -> 218 us (0.43); the launches traced: 493 us -> 217 us
  waiting for transfers between devices: 290 us -> 0 us
  Pallas kernels: 0 us -> 175 us
  matrix products: 62.4 us -> 0 us
  other arithmetic: 44.9 us -> 1.46 us
  local copies, waits for them, and re-layouts: 65.1 us -> 40.7 us
  starting transfers between devices: 16.2 us -> 0 us
  between operations: 14.6 us -> 0.67 us
    pallas_call x0 -> x3, Pallas kernels: none -> 175 us  [the longest x1 82.8 us: split_hidden(): pl.pallas_call(functools.partial(gather_kernel, depth), name='gather_part...]
    all_gather x4 -> x0, waiting for transfers between devices: 154 us -> none  [the longest x1 56.4 us: on_device(): lax.all_gather(weight_in, 'rows', axis=0, tiled=True)]
    reduce_scatter x2 -> x0, waiting for transfers between devices: 131 us -> none  [the longest x1 106 us: on_device(): lax.psum_scatter((jnp.stack([first_term, second_term], axis=1) * loss_sca...]
    dot_general x6 -> x0, matrix products: 62.4 us -> none  [the longest x1 12.4 us: on_device(): jnp.einsum('tcf,tckd->fckd', mix_out, grad_select, preferred_element_type...]
    convert_element_type x4 -> x0, local copies, waits for them, and re-layouts: 33 us -> none  [the longest x1 29.6 us: on_device(): (jnp.stack([first_term, second_term], axis=1) * loss_scale).astype(jnp.bf...]
    convert_element_type x7 -> x1, other arithmetic: 30.3 us -> 1.46 us  [split_hidden(): kern.astype(bf16)]
    reshape x5, local copies, waits for them, and re-layouts: 2.84 us -> 19.7 us  [the longest x1 5.93 us: split_hidden(): weight_in.reshape(rows, all_cols * nnz * block)]
    gather x2 -> x0, local copies, waits for them, and re-layouts: 11.8 us -> none  [the longest x1 6.08 us: on_device(): jnp.take(cot_full.reshape(tok_count, block_count, block_size), flat_rows,...]
  transfers between devices with their start and end apart: 11 -> 0, of which waited for: 8 -> 0; matrix products, arithmetic and copies ran while one was open for 31% -> 0% of each run, Pallas kernels for 0% -> 0%
where the time goes in v1:
time: 218 us; the launch traced here: 217 us
  Pallas kernels  175 us (80%)
  local copies, waits for them, and re-layouts  40.7 us (19%)
    pallas_call x1, Pallas kernels, split_hidden(): pl.pallas_call(functools.partial(gather_kernel, depth), name='gather_part...  82.8 us
    pallas_call x1, Pallas kernels, split_hidden(): pl.pallas_call(functools.partial(scatter_kernel, depth), name='scatter_su...  69.3 us
    pallas_call x1, Pallas kernels, split_hidden(): pl.pallas_call(functools.partial(local_kernel, width, block, cols, nnz),...  22.5 us
    unnamed x16, local copies, waits for them, and re-layouts  19.4 us
    reshape x1, local copies, waits for them, and re-layouts, split_hidden(): weight_in.reshape(rows, all_cols * nnz * block)  5.93 us
    reshape x1, local copies, waits for them, and re-layouts, split_hidden(): weight_out.reshape(rows, all_cols * nnz * block)  5.78 us

profile of v1, /device:TPU:0, one launch (start us, length us, event | category | flops | bytes accessed | tf_op | source)
XLA Modules:
  0.0 217.4 jit_solution(7538199111698674774)
XLA Ops:
  0.6 0.0 copy-start
  0.7 0.8 constant_dynamic-slice_fusion.1
  1.5 0.1 copy.15
  1.6 0.6 reshape.38.ids
  2.2 0.0 copy-done
  2.2 0.6 constant_dynamic-slice_fusion.taps
  2.8 5.0 %copy.16 = bf16[64,16,5,256]{3,2,1,0:T(8,128)(2,1)} copy(bf16[64,16,5,256]{3,1,2,0:T(8,128)(2,1)} %param.8) | data formatting | bytes 5242880 | tf_op args[2]
  7.8 0.0 copy-start.1
  7.8 5.9 %reshape.41.w_in = bf16[64,20480]{1,0:T(8,128)(2,1)} reshape(bf16[64,16,5,256]{3,2,1,0:T(8,128)(2,1)} %copy.16) | data formatting | bytes 5242880 | tf_op jit(solution)/shard_map/reshape | solution.py:403
  13.8 0.0 copy-done.1
  13.8 3.3 %copy.17 = bf16[64,16,5,256]{3,2,1,0:T(8,128)(2,1)} copy(bf16[64,16,5,256]{3,1,2,0:T(8,128)(2,1)S(1)} %copy-done.1) | data formatting | bytes 5242880 | tf_op args[3]
  17.1 5.8 %reshape.42.w_out = bf16[64,20480]{1,0:T(8,128)(2,1)} reshape(bf16[64,16,5,256]{3,2,1,0:T(8,128)(2,1)} %copy.17) | data formatting | bytes 5242880 | tf_op jit(solution)/shard_map/reshape | solution.py:404
  22.8 82.8 %gather_parts.1 = (bf16[512,4096]{1,0:T(8,128)(2,1)}, bf16[512,4096]{1,0:T(8,128)(2,1)}, bf16[256,5120]{1,0:T(8,128)(2,1)}, bf16[256,5120]{1,0:T(8,128)(2,1)}) custom-call(bf16[128,1024]{1,0:T(8,128)(2,1)} %bitcast.4, bf16[128,1024]{1,0:T(8,128)(2,1)} %bitcast.5, bf16[64,20480]{1,0:T(8,128)(2,1)} %reshape.41.w_in, bf16[64,20480]{1,0:T(8,128)(2,1)} %reshape.42.w_out), custom_call_target="tpu_custom_call" | custom-call | tf_op jit(solution)/shard_map/gather_parts/pallas_call | solution.py:386
  105.6 22.5 %local_math.1 = (bf16[512,4096]{1,0:T(8,128)(2,1)}, bf16[256,5120]{1,0:T(8,128)(2,1)}, bf16[256,5120]{1,0:T(8,128)(2,1)}, f32[16,1024]{1,0:T(8,128)}) custom-call(s32[20]{0:T(128)} %reshape.38.ids, bf16[512,4096]{1,0:T(8,128)(2,1)} %get-tuple-element.16.tok, bf16[512,4096]{1,0:T(8,128)(2,1)} %get-tuple-element.17.cot, ...), custom_call_target="tpu_custom_call" | custom-call | tf_op jit(solution)/shard_map/local_math/pallas_call | solution.py:409
  128.1 1.5 convert_element_type.2.kern
  129.6 69.3 %scatter_sums.1 = (bf16[128,1024]{1,0:T(8,128)(2,1)}, bf16[32,20480]{1,0:T(8,128)(2,1)}, bf16[32,20480]{1,0:T(8,128)(2,1)}, f32[16,4096]{1,0:T(8,128)}) custom-call(bf16[512,4096]{1,0:T(8,128)(2,1)} %get-tuple-element.20.dx, bf16[256,5120]{1,0:T(8,128)(2,1)} %get-tuple-element.21.gw_in, bf16[256,5120]{1,0:T(8,128)(2,1)} %get-tuple-element.22.gw_out, ...), custom_call_target="tpu_custom_call" | custom-call | tf_op jit(solution)/shard_map/scatter_sums/pallas_call | solution.py:424
  198.8 4.3 %reshape.49 = f32[32,16,5,256]{3,2,1,0:T(8,128)} reshape(bf16[32,20480]{1,0:T(8,128)(2,1)} %get-tuple-element.25) | data formatting | bytes 3932160 | tf_op jit(solution)/shard_map/reshape | solution.py:456
  203.1 0.0 copy-start.2
  203.1 4.9 %copy.18 = f32[32,16,5,256]{3,1,2,0:T(8,128)} copy(f32[32,16,5,256]{3,2,1,0:T(8,128)} %reshape.49) | data formatting | bytes 5242880
  207.9 0.0 copy-done.2
  208.0 3.2 %reshape.51 = f32[32,16,5,256]{3,2,1,0:T(8,128)} reshape(bf16[32,20480]{1,0:T(8,128)(2,1)S(1)} %copy-done.2) | data formatting | bytes 3932160 | tf_op jit(solution)/shard_map/reshape | solution.py:457
  211.1 0.0 copy-start.4
  211.1 0.0 copy-start.3
  211.1 4.8 %copy.19 = f32[32,16,5,256]{3,1,2,0:T(8,128)} copy(f32[32,16,5,256]{3,2,1,0:T(8,128)} %reshape.51) | data formatting | bytes 5242880
  215.9 0.0 copy-done.4
  215.9 0.7 copy.22
  216.6 0.0 copy-done.3
  216.7 0.7 copy.23
Async XLA Ops:
  0.6 1.5 copy-start
  7.8 5.9 %copy-start.1 = (bf16[64,16,5,256]{3,1,2,0:T(8,128)(2,1)S(1)}, bf16[64,16,5,256]{3,1,2,0:T(8,128)(2,1)}, u32[]{:S(2)}) copy-start(bf16[64,16,5,256]{3,1,2,0:T(8,128)(2,1)} %param.9) | copy-start | bytes 7864324
  203.1 4.9 %copy-start.2 = (bf16[32,20480]{1,0:T(8,128)(2,1)S(1)}, bf16[32,20480]{1,0:T(8,128)(2,1)}, u32[]{:S(2)}) copy-start(bf16[32,20480]{1,0:T(8,128)(2,1)} %get-tuple-element.26) | copy-start | bytes 3932164
  211.1 4.8 %copy-start.4 = (bf16[128,1024]{1,0:T(8,128)(2,1)S(1)}, bf16[128,1024]{1,0:T(8,128)(2,1)}, u32[]{:S(2)}) copy-start(bf16[128,1024]{1,0:T(8,128)(2,1)} %get-tuple-element.24) | copy-start | bytes 786436
  211.1 5.5 %copy-start.3 = (f32[16,4096]{1,0:T(8,128)S(1)}, f32[16,4096]{1,0:T(8,128)}, u32[]{:S(2)}) copy-start(f32[16,4096]{1,0:T(8,128)} %get-tuple-element.27) | copy-start | bytes 786436

commit v2 on v1

--- a/solution.py
+++ b/solution.py
@@ -50,19 +50,27 @@
 
 def gather_kernel(
     depth, tok, cot, w_in, w_out, tok_all, cot_all, in_all, out_all,
-    tok_send, tok_recv, w_send, w_recv, own_sem,
+    raw, flat, stage, tok_send, tok_recv, w_send, w_recv, own_sem, raw_sem,
 ):
     y, r, z, same_chip, across, diagonal = neighbours()
     tokens, features = tok.shape
     rows = w_in.shape[0]
     lanes = in_all.shape[1]
     half = rows // 2
+    block = w_in.shape[2]
+    all_cols = stage.shape[1] // rows
+    nnz = w_in.shape[1] // all_cols
+    loads = [
+        pltpu.make_async_copy(src, raw.at[a], raw_sem.at[a]) for a, src in enumerate((w_in, w_out))
+    ]
+    for load in loads:
+        load.start()
     enter(
         [{"rows": same_chip}, {"rows": across}, {"rows": diagonal}, {"crop": 1 - y}]
         + [{"hid": (z + step) % depth} for step in range(1, depth)]
     )
     streams = ((tok, tok_all), (cot, cot_all))
-    panels = ((w_in, in_all), (w_out, out_all))
+    panels = ((flat.at[0], in_all), (flat.at[1], out_all))
     started, local = [], []
 
     def piece(full, row, col):
@@ -90,8 +98,28 @@
         for step in range(1, depth):
             send_piece(a, src, r, z, step - 1, {"hid": (z + step) % depth})
         send_piece(a, src, r, z, depth - 1, {"rows": across})
+        send_piece(a, src, r, z, depth, {"rows": same_chip})
+        local.append(pltpu.make_async_copy(src, piece(streams[a][1], r, z), own_sem.at[a, 0]))
+        local[-1].start()
+
+    def flatten(a):
+        def turn(k, carry):
+            for h in range(block // 128):
+                part = raw[a, :, span(k, all_cols), h * 128 : (h + 1) * 128]
+                stage[h] = part.astype(jnp.float32).reshape(rows * all_cols, 128)
+            for c in range(all_cols):
+                for h in range(block // 128):
+                    flat[a, :, pl.ds(pl.multiple_of((c * nnz + k) * block + h * 128, 128), 128)] = stage[
+                        h, pl.ds(c, rows, stride=all_cols), :
+                    ].astype(jnp.bfloat16)
+            return carry
+
+        lax.fori_loop(0, nnz, turn, 0)
+
     for a in range(2):
         src, full = panels[a]
+        loads[a].wait()
+        flatten(a)
         for slot, dest in ((1, across), (2, diagonal)):
             copy = remote(
                 src.at[span(y, half), span(dest, lanes)],
@@ -111,15 +139,12 @@
         )
         copy.start()
         started.append(copy)
-        send_piece(a, streams[a][0], r, z, depth, {"rows": same_chip})
-        local.append(pltpu.make_async_copy(streams[a][0], piece(streams[a][1], r, z), own_sem.at[a, 0]))
         local.append(
             pltpu.make_async_copy(
                 src.at[:, span(r, lanes)], full.at[span(r, rows), :], own_sem.at[a, 1]
             )
         )
-    for copy in local:
-        copy.start()
+        local[-1].start()
     for step in range(1, depth):
         col = (z + step) % depth
         for a in range(2):
@@ -174,9 +199,10 @@
 
 def local_kernel(
     width, block, cols, nnz, ids, tok, cot, w_in, w_out, taps,
-    dx_out, gw_in, gw_out, kern, dx, pre_s, act_s, slope_s, mg_s,
+    dx_out, gw_in, gw_out, kern_out, kern, dx, pre_s, act_s, slope_s, mg_s,
 ):
     count = tok.shape[0]
+    me = lax.axis_index("rows")
     dx[...] = jnp.zeros_like(dx)
     place = lax.broadcasted_iota(jnp.int32, (count, block), 0) % width
     kern[...] = jnp.zeros_like(kern)
@@ -198,7 +224,7 @@
         hidden = span(c, block)
 
         def feats(k):
-            return span(ids[c * nnz + k], block)
+            return span(ids[me * cols + c, k], block)
 
         def panel(k):
             return span(c * nnz + k, block)
@@ -220,7 +246,7 @@
 
         def tap(a, b):
             row = 3 * (a + 1) + (b + 1)
-            return taps[row : row + 1, hidden]
+            return taps[row : row + 1, span(me * cols + c, block)]
 
         acts = spread(act_s[...])
         mixed = stack_rows(
@@ -251,6 +277,7 @@
 
     lax.fori_loop(0, cols, column, 0)
     dx_out[...] = dx[...].astype(jnp.bfloat16)
+    kern_out[...] = kern[...].astype(jnp.bfloat16)
 
 
 def scatter_kernel(
@@ -370,6 +397,15 @@
         copy.wait_send()
 
 
+def finish_kernel(all_cols, nnz, in_mine, out_mine, in_grad, out_grad):
+    block = in_grad.shape[2]
+    for src, dst in ((in_mine, in_grad), (out_mine, out_grad)):
+        for c in range(all_cols):
+            for k in range(nnz):
+                at = (c * nnz + k) * block
+                dst[:, k * all_cols + c, :] = src[:, at : at + block].astype(jnp.float32)
+
+
 def split_hidden(tokens, cotangent, weight_in, weight_out, mix_kernel, block_rows):
     n_rows, depth = lax.axis_size("rows"), lax.axis_size("hid")
     _, height, width, features = tokens.shape
@@ -390,22 +426,23 @@
         in_specs=[ANY] * 4,
         out_specs=[ANY] * 4,
         scratch_shapes=[
+            pltpu.VMEM((2, rows, nnz * all_cols, block), bf16),
+            pltpu.VMEM((2, rows, all_cols * nnz * block), bf16),
+            pltpu.VMEM((block // 128, rows * all_cols, 128), f32),
             dma((2, 4 * depth)),
             dma((2, n_rows, depth)),
             dma((2, 5)),
             dma((2, n_rows, 2)),
             dma((2, 2)),
+            dma((2,)),
         ],
-        compiler_params=pltpu.CompilerParams(collective_id=1, has_side_effects=True),
+        compiler_params=params(collective_id=1, has_side_effects=True),
     )(
         tokens.reshape(count, features),
         cotangent.reshape(count, features),
-        weight_in.reshape(rows, all_cols * nnz * block),
-        weight_out.reshape(rows, all_cols * nnz * block),
-    )
-    me = lax.axis_index("rows")
-    taps = lax.dynamic_slice_in_dim(mix_kernel, me * hidden, hidden, axis=1)
-    ids = lax.dynamic_slice_in_dim(block_rows, me * cols, cols, axis=0).reshape(-1)
+        weight_in.transpose(0, 2, 1, 3).reshape(rows, nnz * all_cols, block),
+        weight_out.transpose(0, 2, 1, 3).reshape(rows, nnz * all_cols, block),
+    )
     dx, gw_in, gw_out, kern = pl.pallas_call(
         functools.partial(local_kernel, width, block, cols, nnz),
         name="local_math",
@@ -413,13 +450,14 @@
             sds((whole, model), bf16),
             sds((block, lanes), bf16),
             sds((block, lanes), bf16),
-            sds((16, hidden), f32),
+            sds((16, hidden), bf16),
         ],
         in_specs=[SMEM] + [VMEM] * 5,
         out_specs=[VMEM] * 4,
-        scratch_shapes=[pltpu.VMEM((whole, model), f32)] + [pltpu.VMEM((whole, block), f32)] * 4,
+        scratch_shapes=[pltpu.VMEM((16, hidden), f32), pltpu.VMEM((whole, model), f32)]
+        + [pltpu.VMEM((whole, block), f32)] * 4,
         compiler_params=params(),
-    )(ids, tok_all, cot_all, in_all, out_all, taps)
+    )(block_rows, tok_all, cot_all, in_all, out_all, mix_kernel)
     out_rows = block // (n_rows * lax.axis_size("crop"))
     dx_mine, in_mine, out_mine, kern_all = pl.pallas_call(
         functools.partial(scatter_kernel, depth),
@@ -449,14 +487,23 @@
             dma((2, n_rows)),
         ],
         compiler_params=params(collective_id=2, has_side_effects=True),
-    )(dx, gw_in, gw_out, kern.astype(bf16))
-    shape = (out_rows, all_cols, nnz, block)
-    return (
-        dx_mine.reshape(tokens.shape),
-        in_mine.astype(f32).reshape(shape),
-        out_mine.astype(f32).reshape(shape),
-        kern_all[: mix_kernel.shape[0]],
-    )
+    )(dx, gw_in, gw_out, kern)
+    step = 16
+    flat_spec = pl.BlockSpec((step, all_cols * nnz * block), lambda i: (i, 0))
+    grad_spec = pl.BlockSpec((step, nnz * all_cols, block), lambda i: (i, 0, 0))
+    grads = pl.pallas_call(
+        functools.partial(finish_kernel, all_cols, nnz),
+        name="finish_weights",
+        grid=(out_rows // step,),
+        out_shape=[sds((out_rows, nnz * all_cols, block), f32)] * 2,
+        in_specs=[flat_spec] * 2,
+        out_specs=[grad_spec] * 2,
+        compiler_params=params(),
+    )(in_mine, out_mine)
+    in_grad, out_grad = [
+        grad.reshape(out_rows, nnz, all_cols, block).transpose(0, 2, 1, 3) for grad in grads
+    ]
+    return (dx_mine.reshape(tokens.shape), in_grad, out_grad, kern_all[: mix_kernel.shape[0]])
 
 
 def padded(shard, sides, width):

time: 218 us -> 184 us (0.84)
  local copies, waits for them, and re-layouts: 40.7 us -> 2.77 us
  Pallas kernels: 175 us -> 180 us
    reshape x5 -> x0, local copies, waits for them, and re-layouts: 19.7 us -> none  [the longest x1 5.93 us: split_hidden(): weight_in.reshape(rows, all_cols * nnz * block)]
    unnamed x16 -> x7, local copies, waits for them, and re-layouts: 19.4 us -> 2.77 us
    pallas_call x0 -> x1, Pallas kernels: none -> 5.4 us  [split_hidden(): pl.pallas_call(functools.partial(finish_kernel, all_cols, nnz), name='fin...]
where the time goes in v2:
time: 184 us; the launch traced here: 183 us
  Pallas kernels  180 us (98%)
  local copies, waits for them, and re-layouts  2.77 us (2%)
    pallas_call x1, Pallas kernels, split_hidden(): pl.pallas_call(functools.partial(gather_kernel, depth), name='gather_part...  82.8 us
    pallas_call x1, Pallas kernels, split_hidden(): pl.pallas_call(functools.partial(scatter_kernel, depth), name='scatter_su...  69.4 us
    pallas_call x1, Pallas kernels, split_hidden(): pl.pallas_call(functools.partial(local_kernel, width, block, cols, nnz),...  22.4 us
    pallas_call x1, Pallas kernels, split_hidden(): pl.pallas_call(functools.partial(finish_kernel, all_cols, nnz), name='fin...  5.4 us

profile of v2, /device:TPU:0, one launch (start us, length us, event | category | flops | bytes accessed | tf_op | source)
XLA Modules:
  0.0 183.5 jit_solution(623040236279399701)
XLA Ops:
  0.6 1.4 copy.10.ids
  2.0 82.8 %gather_parts.1 = (bf16[512,4096]{1,0:T(8,128)(2,1)}, bf16[512,4096]{1,0:T(8,128)(2,1)}, bf16[256,5120]{1,0:T(8,128)(2,1)}, bf16[256,5120]{1,0:T(8,128)(2,1)}) custom-call(bf16[128,1024]{1,0:T(8,128)(2,1)} %bitcast.18, bf16[128,1024]{1,0:T(8,128)(2,1)} %bitcast.19, bf16[64,80,256]{2,1,0:T(8,128)(2,1)} %bitcast.16, bf16[64,80,256]{2,1,0:T(8,128)(2,1)} %bitcast.17), custom_call_target="tpu_custom_call" | custom-call | tf_op jit(solution)/shard_map/gather_parts/pallas_call | solution.py:422
  84.8 22.4 %local_math.1 = (bf16[512,4096]{1,0:T(8,128)(2,1)}, bf16[256,5120]{1,0:T(8,128)(2,1)}, bf16[256,5120]{1,0:T(8,128)(2,1)}, bf16[16,1024]{1,0:T(8,128)(2,1)}) custom-call(s32[16,5]{1,0:T(8,128)} %copy.10.ids, bf16[512,4096]{1,0:T(8,128)(2,1)} %get-tuple-element.18.tok, bf16[512,4096]{1,0:T(8,128)(2,1)} %get-tuple-element.19.cot, ...), custom_call_target="tpu_custom_call" | custom-call | tf_op jit(solution)/shard_map/local_math/pallas_call | solution.py:446
  107.2 69.4 %scatter_sums.1 = (bf16[128,1024]{1,0:T(8,128)(2,1)}, bf16[32,20480]{1,0:T(8,128)(2,1)}, bf16[32,20480]{1,0:T(8,128)(2,1)}, f32[16,4096]{1,0:T(8,128)}) custom-call(bf16[512,4096]{1,0:T(8,128)(2,1)} %get-tuple-element.22.dx, bf16[256,5120]{1,0:T(8,128)(2,1)} %get-tuple-element.23.gw_in, bf16[256,5120]{1,0:T(8,128)(2,1)} %get-tuple-element.24.gw_out, ...), custom_call_target="tpu_custom_call" | custom-call | tf_op jit(solution)/shard_map/scatter_sums/pallas_call | solution.py:462
  176.6 0.0 copy-start.1
  176.6 0.0 copy-start
  176.6 5.4 %finish_weights.1 = (f32[32,80,256]{2,1,0:T(8,128)}, f32[32,80,256]{2,1,0:T(8,128)}) custom-call(bf16[32,20480]{1,0:T(8,128)(2,1)} %get-tuple-element.27.in_mine, bf16[32,20480]{1,0:T(8,128)(2,1)} %get-tuple-element.28.out_mine), custom_call_target="tpu_custom_call" | custom-call | tf_op jit(solution)/shard_map/finish_weights/pallas_call | solution.py:494
  182.0 0.0 copy-done.1
  182.0 0.7 copy.13
  182.8 0.0 copy-done
  182.8 0.7 copy.14
Async XLA Ops:
  176.6 5.4 %copy-start.1 = (bf16[128,1024]{1,0:T(8,128)(2,1)S(1)}, bf16[128,1024]{1,0:T(8,128)(2,1)}, u32[]{:S(2)}) copy-start(bf16[128,1024]{1,0:T(8,128)(2,1)} %get-tuple-element.26) | copy-start | bytes 786436
  176.6 6.1 %copy-start = (f32[16,4096]{1,0:T(8,128)S(1)}, f32[16,4096]{1,0:T(8,128)}, u32[]{:S(2)}) copy-start(f32[16,4096]{1,0:T(8,128)} %get-tuple-element.31) | copy-start | bytes 786436

commit v3 on v2

--- a/solution.py
+++ b/solution.py
@@ -71,36 +71,48 @@
     )
     streams = ((tok, tok_all), (cot, cot_all))
     panels = ((flat.at[0], in_all), (flat.at[1], out_all))
-    started, local = [], []
+    targets = ({"hid": z + 1}, {"hid": z - 1}, {"rows": across}, {"rows": same_chip})
+    has_up, has_down = z + 1 < depth, z >= 1
+    sends, local = [], []
+
+    def launch(make, have=None):
+        sends.append((make, have))
+        if have is None:
+            make().start()
+        else:
+            pl.when(have)(lambda: make().start())
 
     def piece(full, row, col):
         return full.at[span(row, tokens), span(col, features)]
 
-    def send_piece(a, src, row, col, slot, target):
-        copy = remote(
-            src, piece(streams[a][1], row, col), tok_send.at[a, slot], tok_recv.at[a, row, col], target
-        )
-        copy.start()
-        started.append(copy)
-
-    def await_piece(a, row, col):
-        part = piece(streams[a][1], row, col)
-        remote(
-            part, part, tok_send.at[a, 0], tok_recv.at[a, row, col], {"rows": same_chip}
-        ).wait_recv()
-        return part
+    def pass_on(a, which, col, kind, have=None, own=False):
+        def make():
+            row = (r, across)[which]
+            part = piece(streams[a][1], row, col)
+            return remote(
+                streams[a][0] if own else part,
+                part,
+                tok_send.at[a, which, col, kind],
+                tok_recv.at[a, row, col],
+                targets[kind],
+            )
+
+        launch(make, have)
+
+    def await_piece(a, row, col, have=None):
+        def wait():
+            part = piece(streams[a][1], row, col)
+            remote(
+                part, part, tok_send.at[a, 0, 0, 3], tok_recv.at[a, row, col], {"rows": same_chip}
+            ).wait_recv()
+
+        if have is None:
+            wait()
+        else:
+            pl.when(have)(wait)
 
     def half_rows(full, row, h):
         return full.at[pl.ds(pl.multiple_of(row * rows + h * half, half), half), :]
-
-    for a in range(2):
-        src = streams[a][0]
-        for step in range(1, depth):
-            send_piece(a, src, r, z, step - 1, {"hid": (z + step) % depth})
-        send_piece(a, src, r, z, depth - 1, {"rows": across})
-        send_piece(a, src, r, z, depth, {"rows": same_chip})
-        local.append(pltpu.make_async_copy(src, piece(streams[a][1], r, z), own_sem.at[a, 0]))
-        local[-1].start()
 
     def flatten(a):
         def turn(k, carry):
@@ -116,59 +128,78 @@
 
         lax.fori_loop(0, nnz, turn, 0)
 
-    for a in range(2):
+    def give_weights(a):
         src, full = panels[a]
         loads[a].wait()
         flatten(a)
         for slot, dest in ((1, across), (2, diagonal)):
-            copy = remote(
-                src.at[span(y, half), span(dest, lanes)],
-                half_rows(full, r, y),
-                w_send.at[a, slot],
-                w_recv.at[a, r, y],
-                {"rows": dest},
-            )
-            copy.start()
-            started.append(copy)
-        copy = remote(
-            src.at[:, span(same_chip, lanes)],
-            full.at[span(r, rows), :],
-            w_send.at[a, 0],
-            w_recv.at[a, r, 0],
-            {"rows": same_chip},
-        )
-        copy.start()
-        started.append(copy)
-        local.append(
-            pltpu.make_async_copy(
-                src.at[:, span(r, lanes)], full.at[span(r, rows), :], own_sem.at[a, 1]
-            )
-        )
-        local[-1].start()
-    for step in range(1, depth):
-        col = (z + step) % depth
-        for a in range(2):
-            part = await_piece(a, r, col)
-            send_piece(a, part, r, col, depth + 2 * step - 1, {"rows": across})
-            send_piece(a, part, r, col, depth + 2 * step, {"rows": same_chip})
-    for a in range(2):
+            launch(
+                lambda slot=slot, dest=dest: remote(
+                    src.at[span(y, half), span(dest, lanes)],
+                    half_rows(full, r, y),
+                    w_send.at[a, slot],
+                    w_recv.at[a, r, y],
+                    {"rows": dest},
+                )
+            )
+        launch(
+            lambda: remote(
+                src.at[:, span(same_chip, lanes)],
+                full.at[span(r, rows), :],
+                w_send.at[a, 0],
+                w_recv.at[a, r, 0],
+                {"rows": same_chip},
+            )
+        )
+        keep = pltpu.make_async_copy(
+            src.at[:, span(r, lanes)], full.at[span(r, rows), :], own_sem.at[a, 1]
+        )
+        keep.start()
+        local.append(keep)
+
+    def mirror_weights(a):
         full = panels[a][1]
         for slot, row in ((3, across), (4, diagonal)):
             part = half_rows(full, row, y)
-            copy = remote(
-                part, part, w_send.at[a, slot], w_recv.at[a, row, y], {"rows": row}
-            )
-            copy.wait_recv()
-            copy = remote(
-                part, part, w_send.at[a, slot], w_recv.at[a, row, y], {"crop": 1 - y}
-            )
-            copy.start()
-            started.append(copy)
+            remote(part, part, w_send.at[a, slot], w_recv.at[a, row, y], {"rows": row}).wait_recv()
+            launch(
+                lambda slot=slot, row=row, part=part: remote(
+                    part, part, w_send.at[a, slot], w_recv.at[a, row, y], {"crop": 1 - y}
+                )
+            )
+
+    def line_step(step):
+        for below in (True, False):
+            col = z - step if below else z + step
+            have = col >= 0 if below else col < depth
+            onward = jnp.logical_and(have, has_up if below else has_down)
+            for a, which in ((0, 0), (1, 0), (1, 1)):
+                await_piece(a, (r, across)[which], col, have)
+                pass_on(a, which, col, 0 if below else 1, onward)
+                if a == 0:
+                    pass_on(a, which, col, 2, have)
+                pass_on(a, which, col, 3, have)
+
+    for a, kind in ((1, 2), (0, 0), (0, 1), (1, 0), (1, 1), (0, 2), (0, 3), (1, 3)):
+        pass_on(a, 0, z, kind, (has_up, has_down, None, None)[kind], own=True)
+    for a in range(2):
+        keep = pltpu.make_async_copy(streams[a][0], piece(streams[a][1], r, z), own_sem.at[a, 0])
+        keep.start()
+        local.append(keep)
+    give_weights(0)
+    await_piece(1, across, z)
+    for kind in (0, 1, 3):
+        pass_on(1, 1, z, kind, (has_up, has_down, None, None)[kind])
+    give_weights(1)
+    for step in range(1, depth - 1):
+        line_step(step)
+    for a in range(2):
+        mirror_weights(a)
+    line_step(depth - 1)
     for step in range(depth):
         col = (z + step) % depth
-        for a in range(2):
-            part = await_piece(a, across, col)
-            send_piece(a, part, across, col, 3 * depth - 1 + step, {"rows": same_chip})
+        await_piece(0, across, col)
+        pass_on(0, 1, col, 3)
     for a in range(2):
         full = panels[a][1]
         part = full.at[span(same_chip, rows), :]
@@ -185,8 +216,11 @@
                 await_piece(a, row, (z + step) % depth)
     for copy in local:
         copy.wait()
-    for copy in started:
-        copy.wait_send()
+    for make, have in sends:
+        if have is None:
+            make().wait_send()
+        else:
+            pl.when(have)(lambda make=make: make().wait_send())
 
 
 def nt(a, b):
@@ -429,7 +463,7 @@
             pltpu.VMEM((2, rows, nnz * all_cols, block), bf16),
             pltpu.VMEM((2, rows, all_cols * nnz * block), bf16),
             pltpu.VMEM((block // 128, rows * all_cols, 128), f32),
-            dma((2, 4 * depth)),
+            dma((2, 2, depth, 4)),
             dma((2, n_rows, depth)),
             dma((2, 5)),
             dma((2, n_rows, 2)),

time: 184 us -> 172 us (0.935)
  Pallas kernels: 180 us -> 169 us
    pallas_call x1, Pallas kernels: 82.8 us -> 72.1 us  [split_hidden(): pl.pallas_call(functools.partial(gather_kernel, depth), name='gather_part...]
where the time goes in v3:
time: 172 us
  Pallas kernels  169 us (98%)
  local copies, waits for them, and re-layouts  2.77 us (2%)
    pallas_call x1, Pallas kernels, split_hidden(): pl.pallas_call(functools.partial(gather_kernel, depth), name='gather_part...  72.1 us
    pallas_call x1, Pallas kernels, split_hidden(): pl.pallas_call(functools.partial(scatter_kernel, depth), name='scatter_su...  68.8 us
    pallas_call x1, Pallas kernels, split_hidden(): pl.pallas_call(functools.partial(local_kernel, width, block, cols, nnz),...  22.5 us
    pallas_call x1, Pallas kernels, split_hidden(): pl.pallas_call(functools.partial(finish_kernel, all_cols, nnz), name='fin...  5.4 us

profile of v3, /device:TPU:0, one launch (start us, length us, event | category | flops | bytes accessed | tf_op | source)
XLA Modules:
  0.0 172.3 jit_solution(10136115458987059736)
XLA Ops:
  0.6 1.4 copy.10.ids
  2.0 72.1 %gather_parts.1 = (bf16[512,4096]{1,0:T(8,128)(2,1)}, bf16[512,4096]{1,0:T(8,128)(2,1)}, bf16[256,5120]{1,0:T(8,128)(2,1)}, bf16[256,5120]{1,0:T(8,128)(2,1)}) custom-call(bf16[128,1024]{1,0:T(8,128)(2,1)} %bitcast.18, bf16[128,1024]{1,0:T(8,128)(2,1)} %bitcast.19, bf16[64,80,256]{2,1,0:T(8,128)(2,1)} %bitcast.16, bf16[64,80,256]{2,1,0:T(8,128)(2,1)} %bitcast.17), custom_call_target="tpu_custom_call" | custom-call | tf_op jit(solution)/shard_map/gather_parts/pallas_call | solution.py:456
  74.1 22.5 %local_math.1 = (bf16[512,4096]{1,0:T(8,128)(2,1)}, bf16[256,5120]{1,0:T(8,128)(2,1)}, bf16[256,5120]{1,0:T(8,128)(2,1)}, bf16[16,1024]{1,0:T(8,128)(2,1)}) custom-call(s32[16,5]{1,0:T(8,128)} %copy.10.ids, bf16[512,4096]{1,0:T(8,128)(2,1)} %get-tuple-element.18.tok, bf16[512,4096]{1,0:T(8,128)(2,1)} %get-tuple-element.19.cot, ...), custom_call_target="tpu_custom_call" | custom-call | tf_op jit(solution)/shard_map/local_math/pallas_call | solution.py:480
  96.6 68.8 %scatter_sums.1 = (bf16[128,1024]{1,0:T(8,128)(2,1)}, bf16[32,20480]{1,0:T(8,128)(2,1)}, bf16[32,20480]{1,0:T(8,128)(2,1)}, f32[16,4096]{1,0:T(8,128)}) custom-call(bf16[512,4096]{1,0:T(8,128)(2,1)} %get-tuple-element.22.dx, bf16[256,5120]{1,0:T(8,128)(2,1)} %get-tuple-element.23.gw_in, bf16[256,5120]{1,0:T(8,128)(2,1)} %get-tuple-element.24.gw_out, ...), custom_call_target="tpu_custom_call" | custom-call | tf_op jit(solution)/shard_map/scatter_sums/pallas_call | solution.py:496
  165.4 0.0 copy-start.1
  165.4 0.0 copy-start
  165.5 5.4 %finish_weights.1 = (f32[32,80,256]{2,1,0:T(8,128)}, f32[32,80,256]{2,1,0:T(8,128)}) custom-call(bf16[32,20480]{1,0:T(8,128)(2,1)} %get-tuple-element.27.in_mine, bf16[32,20480]{1,0:T(8,128)(2,1)} %get-tuple-element.28.out_mine), custom_call_target="tpu_custom_call" | custom-call | tf_op jit(solution)/shard_map/finish_weights/pallas_call | solution.py:528
  170.9 0.0 copy-done.1
  170.9 0.7 copy.13
  171.6 0.0 copy-done
  171.6 0.7 copy.14
Async XLA Ops:
  165.4 5.4 %copy-start.1 = (bf16[128,1024]{1,0:T(8,128)(2,1)S(1)}, bf16[128,1024]{1,0:T(8,128)(2,1)}, u32[]{:S(2)}) copy-start(bf16[128,1024]{1,0:T(8,128)(2,1)} %get-tuple-element.26) | copy-start | bytes 786436
  165.4 6.1 %copy-start = (f32[16,4096]{1,0:T(8,128)S(1)}, f32[16,4096]{1,0:T(8,128)}, u32[]{:S(2)}) copy-start(f32[16,4096]{1,0:T(8,128)} %get-tuple-element.31) | copy-start | bytes 786436

commit v4 on v3

--- a/solution.py
+++ b/solution.py
@@ -237,9 +237,13 @@
 ):
     count = tok.shape[0]
     me = lax.axis_index("rows")
-    dx[...] = jnp.zeros_like(dx)
+    c = pl.program_id(0)
     place = lax.broadcasted_iota(jnp.int32, (count, block), 0) % width
-    kern[...] = jnp.zeros_like(kern)
+
+    @pl.when(c == 0)
+    def _():
+        dx[...] = jnp.zeros_like(dx)
+        kern[...] = jnp.zeros_like(kern)
 
     def spread(value):
         before = jnp.where(place == 0, 0.0, pltpu.roll(value, 1, 0))
@@ -254,73 +258,77 @@
             + jnp.concatenate([down[width:], edge], axis=0)
         )
 
-    def column(c, carry):
-        hidden = span(c, block)
-
-        def feats(k):
-            return span(ids[me * cols + c, k], block)
-
-        def panel(k):
-            return span(c * nnz + k, block)
-
-        pre = jnp.dot(tok[:, feats(0)], w_in[:, panel(0)], preferred_element_type=jnp.float32)
-        for k in range(1, nnz):
-            pre += jnp.dot(tok[:, feats(k)], w_in[:, panel(k)], preferred_element_type=jnp.float32)
-        pre_s[...] = pre
-        mg = nt(cot[:, feats(0)], w_out[:, panel(0)])
-        for k in range(1, nnz):
-            mg += nt(cot[:, feats(k)], w_out[:, panel(k)])
-        mg_s[...] = mg.astype(jnp.bfloat16).astype(jnp.float32)
-        p = pre_s[...]
-        t = jnp.tanh(root_two_pi * (p + cubic_coef * p * p * p))
-        act_s[...] = (0.5 * p * (1.0 + t)).astype(jnp.bfloat16).astype(jnp.float32)
-        slope_s[...] = 0.5 * (1.0 + t) + 0.5 * p * (1.0 - t * t) * root_two_pi * (
-            1.0 + 3.0 * cubic_coef * p * p
+    hidden = span(c, block)
+
+    def feats(k):
+        return span(ids[k, me * cols + c], block)
+
+    def panel(k):
+        return slice(k * block, (k + 1) * block)
+
+    pre = jnp.dot(tok[:, feats(0)], w_in[:, panel(0)], preferred_element_type=jnp.float32)
+    for k in range(1, nnz):
+        pre += jnp.dot(tok[:, feats(k)], w_in[:, panel(k)], preferred_element_type=jnp.float32)
+    pre_s[...] = pre
+    mg = nt(cot[:, feats(0)], w_out[:, panel(0)])
+    for k in range(1, nnz):
+        mg += nt(cot[:, feats(k)], w_out[:, panel(k)])
+    mg_s[...] = mg.astype(jnp.bfloat16).astype(jnp.float32)
+    p = pre_s[...]
+    t = jnp.tanh(root_two_pi * (p + cubic_coef * p * p * p))
+    act_s[...] = (0.5 * p * (1.0 + t)).astype(jnp.bfloat16).astype(jnp.float32)
+    slope_s[...] = 0.5 * (1.0 + t) + 0.5 * p * (1.0 - t * t) * root_two_pi * (
+        1.0 + 3.0 * cubic_coef * p * p
+    )
+
+    def tap(a, b):
+        row = 3 * (a + 1) + (b + 1)
+        return taps[row : row + 1, span(me * cols + c, block)]
+
+    acts = spread(act_s[...])
+    mixed = stack_rows(
+        *[sum(tap(a, b) * acts[b + 1] for b in (-1, 0, 1)) for a in (-1, 0, 1)]
+    ).astype(jnp.bfloat16)
+    grads = mg_s[...]
+    for b in (-1, 0, 1):
+        seen = acts[b + 1]
+        sums = (
+            jnp.sum(seen[:-width] * grads[width:], axis=0, keepdims=True),
+            jnp.sum(seen * grads, axis=0, keepdims=True),
+            jnp.sum(seen[width:] * grads[:-width], axis=0, keepdims=True),
         )
-
-        def tap(a, b):
+        for a in (-1, 0, 1):
             row = 3 * (a + 1) + (b + 1)
-            return taps[row : row + 1, span(me * cols + c, block)]
-
-        acts = spread(act_s[...])
-        mixed = stack_rows(
-            *[sum(tap(a, b) * acts[b + 1] for b in (-1, 0, 1)) for a in (-1, 0, 1)]
-        ).astype(jnp.bfloat16)
-        grads = mg_s[...]
-        for b in (-1, 0, 1):
-            seen = acts[b + 1]
-            sums = (
-                jnp.sum(seen[:-width] * grads[width:], axis=0, keepdims=True),
-                jnp.sum(seen * grads, axis=0, keepdims=True),
-                jnp.sum(seen[width:] * grads[:-width], axis=0, keepdims=True),
-            )
-            for a in (-1, 0, 1):
-                row = 3 * (a + 1) + (b + 1)
-                kern[row : row + 1, hidden] = sums[a + 1] * loss_scale
-        for k in range(nnz):
-            gw_out[:, panel(k)] = (tn(mixed, cot[:, feats(k)]) * loss_scale).astype(jnp.bfloat16)
-        backs = spread(mg_s[...])
-        gathered = stack_rows(
-            *[sum(tap(a, b) * backs[1 - b] for b in (-1, 0, 1)) for a in (1, 0, -1)]
-        )
-        pre_grad = (gathered * slope_s[...]).astype(jnp.bfloat16)
-        for k in range(nnz):
-            gw_in[:, panel(k)] = (tn(tok[:, feats(k)], pre_grad) * loss_scale).astype(jnp.bfloat16)
-            dx[:, feats(k)] += nt(pre_grad, w_in[:, panel(k)])
-        return carry
-
-    lax.fori_loop(0, cols, column, 0)
-    dx_out[...] = dx[...].astype(jnp.bfloat16)
-    kern_out[...] = kern[...].astype(jnp.bfloat16)
+            kern[row : row + 1, hidden] = sums[a + 1] * loss_scale
+    for k in range(nnz):
+        gw_out[:, panel(k)] = (tn(mixed, cot[:, feats(k)]) * loss_scale).astype(jnp.bfloat16)
+    backs = spread(mg_s[...])
+    gathered = stack_rows(
+        *[sum(tap(a, b) * backs[1 - b] for b in (-1, 0, 1)) for a in (1, 0, -1)]
+    )
+    pre_grad = (gathered * slope_s[...]).astype(jnp.bfloat16)
+    for k in range(nnz):
+        gw_in[:, panel(k)] = (tn(tok[:, feats(k)], pre_grad) * loss_scale).astype(jnp.bfloat16)
+        dx[:, feats(k)] += nt(pre_grad, w_in[:, panel(k)])
+
+    @pl.when(c == cols - 1)
+    def _():
+        dx_out[...] = dx[...].astype(jnp.bfloat16)
+        kern_out[...] = kern[...].astype(jnp.bfloat16)
 
 
 def scatter_kernel(
     depth, dx, gw_in, gw_out, kern, dx_mine, in_mine, out_mine, kern_all,
-    dx_near, dx_half, dx_far, dx_sum, dx_last, gw_part, gw_sum, kern_part,
-    dx_send, dx_recv, gw_send, gw_recv, kern_send, kern_recv,
+    dx_own, gw_own, dx_near, dx_half, dx_far, dx_sum, dx_last, gw_part, gw_sum, kern_part,
+    dx_send, dx_recv, gw_send, gw_recv, kern_send, kern_recv, dx_load, gw_load,
 ):
     y, r, z, same_chip, across, diagonal = neighbours()
     group = [same_chip, across, diagonal]
+    order = (across, diagonal, same_chip, r)
+    tokens, features = dx_mine.shape
+    rows = in_mine.shape[0]
+    lanes = gw_in.shape[1]
+    weights = ((gw_in, in_mine), (gw_out, out_mine))
     enter(
         [{"rows": row} for row in group]
         + [{"crop": 1 - y, "rows": row} for row in group]
@@ -334,13 +342,8 @@
         copy.start()
         started.append(copy)
 
-    tokens, features = dx_mine.shape
-    rows = in_mine.shape[0]
-    lanes = gw_in.shape[1]
-    weights = ((gw_in, in_mine), (gw_out, out_mine))
     for slot, row in enumerate((diagonal, same_chip)):
         go(dx.at[span(row, tokens), :], dx_near.at[slot], dx_send.at[slot], dx_recv.at[slot], {"rows": same_chip})
-    order = (across, diagonal, same_chip, r)
     for slot, row in enumerate(order):
         for a in range(2):
             go(
@@ -350,6 +353,21 @@
                 gw_recv.at[a, slot],
                 {"crop": 1 - y},
             )
+    dx_loads = [
+        pltpu.make_async_copy(dx.at[span(row, tokens), :], dx_own.at[slot], dx_load.at[slot])
+        for slot, row in enumerate((across, r))
+    ]
+    gw_loads = [
+        [
+            pltpu.make_async_copy(
+                weights[a][0].at[span(y * 4 + row, rows), :], gw_own.at[a, slot], gw_load.at[a, slot]
+            )
+            for a in range(2)
+        ]
+        for slot, row in enumerate(order)
+    ]
+    for load in dx_loads + [load for pair in gw_loads for load in pair]:
+        load.start()
     for slot, row in enumerate(group):
         go(kern, kern_part.at[y, r], kern_send.at[slot], kern_recv.at[y, r], {"rows": row})
         go(
@@ -365,16 +383,18 @@
         remote(ref, ref, send_sem, recv_sem, target).wait_recv()
 
     arrived(dx_near.at[0], dx_send.at[0], dx_recv.at[0], {"rows": same_chip})
+    dx_loads[0].wait()
     dx_half[...] = (
-        dx[span(across, tokens), :].astype(jnp.float32) + dx_near[0].astype(jnp.float32)
+        dx_own[0].astype(jnp.float32) + dx_near[0].astype(jnp.float32)
     ).astype(jnp.bfloat16)
     go(dx_half, dx_far, dx_send.at[2], dx_recv.at[2], {"rows": across})
     arrived(dx_near.at[1], dx_send.at[1], dx_recv.at[1], {"rows": same_chip})
     arrived(dx_far, dx_send.at[2], dx_recv.at[2], {"rows": across})
+    dx_loads[1].wait()
     for col in range(depth):
         part = slice(col * features, (col + 1) * features)
         dx_sum[col] = (
-            dx[span(r, tokens), part].astype(jnp.float32)
+            dx_own[1, :, part].astype(jnp.float32)
             + dx_near[1, :, part].astype(jnp.float32)
             + dx_far[:, part].astype(jnp.float32)
         ).astype(jnp.bfloat16)
@@ -389,8 +409,9 @@
     for slot, row in enumerate(order):
         for a in range(2):
             arrived(gw_part.at[a, slot], gw_send.at[a, slot], gw_recv.at[a, slot], {"crop": 1 - y})
+            gw_loads[slot][a].wait()
             total = (
-                weights[a][0][span(y * 4 + row, rows), :].astype(jnp.float32)
+                gw_own[a, slot].astype(jnp.float32)
                 + gw_part[a, slot].astype(jnp.float32)
             ).astype(jnp.bfloat16)
             if slot == 3:
@@ -431,8 +452,12 @@
         copy.wait_send()
 
 
-def finish_kernel(all_cols, nnz, in_mine, out_mine, in_grad, out_grad):
+def finish_kernel(
+    all_cols, nnz, in_mine, out_mine, dx_mine, kern_all, in_grad, out_grad, dx_grad, kern_grad
+):
     block = in_grad.shape[2]
+    dx_grad[...] = dx_mine[...]
+    kern_grad[...] = kern_all[: kern_grad.shape[0]]
     for src, dst in ((in_mine, in_grad), (out_mine, out_grad)):
         for c in range(all_cols):
             for k in range(nnz):
@@ -477,6 +502,7 @@
         weight_in.transpose(0, 2, 1, 3).reshape(rows, nnz * all_cols, block),
         weight_out.transpose(0, 2, 1, 3).reshape(rows, nnz * all_cols, block),
     )
+    panel_spec = pl.BlockSpec((block, nnz * block), lambda c: (0, c))
     dx, gw_in, gw_out, kern = pl.pallas_call(
         functools.partial(local_kernel, width, block, cols, nnz),
         name="local_math",
@@ -486,12 +512,13 @@
             sds((block, lanes), bf16),
             sds((16, hidden), bf16),
         ],
-        in_specs=[SMEM] + [VMEM] * 5,
-        out_specs=[VMEM] * 4,
+        grid=(cols,),
+        in_specs=[SMEM, VMEM, VMEM, panel_spec, panel_spec, VMEM],
+        out_specs=[VMEM, panel_spec, panel_spec, VMEM],
         scratch_shapes=[pltpu.VMEM((16, hidden), f32), pltpu.VMEM((whole, model), f32)]
         + [pltpu.VMEM((whole, block), f32)] * 4,
         compiler_params=params(),
-    )(block_rows, tok_all, cot_all, in_all, out_all, mix_kernel)
+    )(block_rows.T, tok_all, cot_all, in_all, out_all, mix_kernel)
     out_rows = block // (n_rows * lax.axis_size("crop"))
     dx_mine, in_mine, out_mine, kern_all = pl.pallas_call(
         functools.partial(scatter_kernel, depth),
@@ -502,9 +529,11 @@
             sds((out_rows, all_cols * nnz * block), bf16),
             sds((16, hidden * n_rows), f32),
         ],
-        in_specs=[VMEM] * 4,
+        in_specs=[ANY] * 3 + [VMEM],
         out_specs=[VMEM] * 4,
         scratch_shapes=[
+            pltpu.VMEM((2, count, model), bf16),
+            pltpu.VMEM((2, 4, out_rows, lanes), bf16),
             pltpu.VMEM((2, count, model), bf16),
             pltpu.VMEM((count, model), bf16),
             pltpu.VMEM((count, model), bf16),
@@ -519,25 +548,29 @@
             dma((2, 7)),
             dma((7,)),
             dma((2, n_rows)),
+            dma((2,)),
+            dma((2, 4)),
         ],
         compiler_params=params(collective_id=2, has_side_effects=True),
     )(dx, gw_in, gw_out, kern)
-    step = 16
+    step = 8
+    part = pl.BlockSpec((count * step // out_rows, features), lambda i: (i, 0))
     flat_spec = pl.BlockSpec((step, all_cols * nnz * block), lambda i: (i, 0))
     grad_spec = pl.BlockSpec((step, nnz * all_cols, block), lambda i: (i, 0, 0))
-    grads = pl.pallas_call(
+    in_grad, out_grad, dx_grad, kern_grad = pl.pallas_call(
         functools.partial(finish_kernel, all_cols, nnz),
         name="finish_weights",
         grid=(out_rows // step,),
-        out_shape=[sds((out_rows, nnz * all_cols, block), f32)] * 2,
-        in_specs=[flat_spec] * 2,
-        out_specs=[grad_spec] * 2,
+        out_shape=[sds((out_rows, nnz * all_cols, block), f32)] * 2
+        + [sds((count, features), bf16), sds(mix_kernel.shape, f32)],
+        in_specs=[flat_spec] * 2 + [part, VMEM],
+        out_specs=[grad_spec] * 2 + [part, VMEM],
         compiler_params=params(),
-    )(in_mine, out_mine)
+    )(in_mine, out_mine, dx_mine, kern_all)
     in_grad, out_grad = [
-        grad.reshape(out_rows, nnz, all_cols, block).transpose(0, 2, 1, 3) for grad in grads
+        grad.reshape(out_rows, nnz, all_cols, block).transpose(0, 2, 1, 3) for grad in (in_grad, out_grad)
     ]
-    return (dx_mine.reshape(tokens.shape), in_grad, out_grad, kern_all[: mix_kernel.shape[0]])
+    return (dx_grad.reshape(tokens.shape), in_grad, out_grad, kern_grad)
 
 
 def padded(shard, sides, width):

time: 172 us -> 166 us (0.965)
  Pallas kernels: 169 us -> 165 us
  local copies, waits for them, and re-layouts: 2.77 us -> 0 us
    unnamed x7 -> x0, local copies, waits for them, and re-layouts: 2.77 us -> none
    pallas_call x1, Pallas kernels: 68.8 us -> 66.2 us  [split_hidden(): pl.pallas_call(functools.partial(scatter_kernel, depth), name='scatter_su...]
    pallas_call x1, Pallas kernels: 22.5 us -> 20.8 us  [split_hidden(): pl.pallas_call(functools.partial(local_kernel, width, block, cols, nnz),...]
where the time goes in v4:
time: 166 us
  Pallas kernels  165 us (99%)
    pallas_call x1, Pallas kernels, split_hidden(): pl.pallas_call(functools.partial(gather_kernel, depth), name='gather_part...  72.2 us
    pallas_call x1, Pallas kernels, split_hidden(): pl.pallas_call(functools.partial(scatter_kernel, depth), name='scatter_su...  66.2 us
    pallas_call x1, Pallas kernels, split_hidden(): pl.pallas_call(functools.partial(local_kernel, width, block, cols, nnz),...  20.8 us
    pallas_call x1, Pallas kernels, split_hidden(): pl.pallas_call(functools.partial(finish_kernel, all_cols, nnz), name='fin...  5.91 us

profile of v4, /device:TPU:0, one launch (start us, length us, event | category | flops | bytes accessed | tf_op | source)
XLA Modules:
  0.0 165.7 jit_solution(8923066169136176399)
XLA Ops:
  0.6 72.2 %gather_parts.1 = (bf16[512,4096]{1,0:T(8,128)(2,1)}, bf16[512,4096]{1,0:T(8,128)(2,1)}, bf16[256,5120]{1,0:T(8,128)(2,1)}, bf16[256,5120]{1,0:T(8,128)(2,1)}) custom-call(bf16[128,1024]{1,0:T(8,128)(2,1)} %bitcast.18, bf16[128,1024]{1,0:T(8,128)(2,1)} %bitcast.19, bf16[64,80,256]{2,1,0:T(8,128)(2,1)} %bitcast.16, bf16[64,80,256]{2,1,0:T(8,128)(2,1)} %bitcast.17), custom_call_target="tpu_custom_call" | custom-call | tf_op jit(solution)/shard_map/gather_parts/pallas_call | solution.py:481
  72.8 20.8 %local_math.1 = (bf16[512,4096]{1,0:T(8,128)(2,1)}, bf16[256,5120]{1,0:T(8,128)(2,1)}, bf16[256,5120]{1,0:T(8,128)(2,1)}, bf16[16,1024]{1,0:T(8,128)(2,1)}) custom-call(s32[5,16]{1,0:T(8,128)} %bitcast.20, bf16[512,4096]{1,0:T(8,128)(2,1)} %get-tuple-element.20.tok, bf16[512,4096]{1,0:T(8,128)(2,1)} %get-tuple-element.21.cot, ...), custom_call_target="tpu_custom_call" | custom-call | tf_op jit(solution)/shard_map/local_math/pallas_call | solution.py:506
  93.6 66.2 %scatter_sums.1 = (bf16[128,1024]{1,0:T(8,128)(2,1)}, bf16[32,20480]{1,0:T(8,128)(2,1)}, bf16[32,20480]{1,0:T(8,128)(2,1)}, f32[16,4096]{1,0:T(8,128)}) custom-call(bf16[512,4096]{1,0:T(8,128)(2,1)} %get-tuple-element.24.dx, bf16[256,5120]{1,0:T(8,128)(2,1)} %get-tuple-element.25.gw_in, bf16[256,5120]{1,0:T(8,128)(2,1)} %get-tuple-element.26.gw_out, ...), custom_call_target="tpu_custom_call" | custom-call | tf_op jit(solution)/shard_map/scatter_sums/pallas_call | solution.py:523
  159.8 5.9 %finish_weights.1 = (f32[32,80,256]{2,1,0:T(8,128)}, f32[32,80,256]{2,1,0:T(8,128)}, bf16[128,1024]{1,0:T(8,128)(2,1)}, f32[9,4096]{1,0:T(8,128)}) custom-call(bf16[32,20480]{1,0:T(8,128)(2,1)} %get-tuple-element.28.in_mine, bf16[32,20480]{1,0:T(8,128)(2,1)} %get-tuple-element.29.out_mine, bf16[128,1024]{1,0:T(8,128)(2,1)} %get-tuple-element.30.dx_mine, ...), custom_call_target="tpu_custom_call" | custom-call | tf_op jit(solution)/shard_map/finish_weights/pallas_call | solution.py:560

commit v5 on v4

--- a/solution.py
+++ b/solution.py
@@ -191,11 +191,12 @@
     for kind in (0, 1, 3):
         pass_on(1, 1, z, kind, (has_up, has_down, None, None)[kind])
     give_weights(1)
-    for step in range(1, depth - 1):
+    for step in range(1, depth):
         line_step(step)
-    for a in range(2):
+        if step <= 2:
+            mirror_weights(step - 1)
+    for a in range(depth - 1, 2):
         mirror_weights(a)
-    line_step(depth - 1)
     for step in range(depth):
         col = (z + step) % depth
         await_piece(0, across, col)

time: 166 us -> 161 us (0.970)
  Pallas kernels: 165 us -> 160 us
    pallas_call x1, Pallas kernels: 72.2 us -> 66.2 us  [split_hidden(): pl.pallas_call(functools.partial(gather_kernel, depth), name='gather_part...]
where the time goes in v5:
time: 161 us; the launch traced here: 160 us
  Pallas kernels  160 us (99%)
    pallas_call x1, Pallas kernels, split_hidden(): pl.pallas_call(functools.partial(scatter_kernel, depth), name='scatter_su...  66.7 us
    pallas_call x1, Pallas kernels, split_hidden(): pl.pallas_call(functools.partial(gather_kernel, depth), name='gather_part...  66.2 us
    pallas_call x1, Pallas kernels, split_hidden(): pl.pallas_call(functools.partial(local_kernel, width, block, cols, nnz),...  20.8 us
    pallas_call x1, Pallas kernels, split_hidden(): pl.pallas_call(functools.partial(finish_kernel, all_cols, nnz), name='fin...  5.91 us

profile of v5, /device:TPU:0, one launch (start us, length us, event | category | flops | bytes accessed | tf_op | source)
XLA Modules:
  0.0 160.3 jit_solution(13209565692293623966)
XLA Ops:
  0.6 66.2 %gather_parts.1 = (bf16[512,4096]{1,0:T(8,128)(2,1)}, bf16[512,4096]{1,0:T(8,128)(2,1)}, bf16[256,5120]{1,0:T(8,128)(2,1)}, bf16[256,5120]{1,0:T(8,128)(2,1)}) custom-call(bf16[128,1024]{1,0:T(8,128)(2,1)} %bitcast.18, bf16[128,1024]{1,0:T(8,128)(2,1)} %bitcast.19, bf16[64,80,256]{2,1,0:T(8,128)(2,1)} %bitcast.16, bf16[64,80,256]{2,1,0:T(8,128)(2,1)} %bitcast.17), custom_call_target="tpu_custom_call" | custom-call | tf_op jit(solution)/shard_map/gather_parts/pallas_call | solution.py:482
  66.8 20.8 %local_math.1 = (bf16[512,4096]{1,0:T(8,128)(2,1)}, bf16[256,5120]{1,0:T(8,128)(2,1)}, bf16[256,5120]{1,0:T(8,128)(2,1)}, bf16[16,1024]{1,0:T(8,128)(2,1)}) custom-call(s32[5,16]{1,0:T(8,128)} %bitcast.20, bf16[512,4096]{1,0:T(8,128)(2,1)} %get-tuple-element.20.tok, bf16[512,4096]{1,0:T(8,128)(2,1)} %get-tuple-element.21.cot, ...), custom_call_target="tpu_custom_call" | custom-call | tf_op jit(solution)/shard_map/local_math/pallas_call | solution.py:507
  87.7 66.7 %scatter_sums.1 = (bf16[128,1024]{1,0:T(8,128)(2,1)}, bf16[32,20480]{1,0:T(8,128)(2,1)}, bf16[32,20480]{1,0:T(8,128)(2,1)}, f32[16,4096]{1,0:T(8,128)}) custom-call(bf16[512,4096]{1,0:T(8,128)(2,1)} %get-tuple-element.24.dx, bf16[256,5120]{1,0:T(8,128)(2,1)} %get-tuple-element.25.gw_in, bf16[256,5120]{1,0:T(8,128)(2,1)} %get-tuple-element.26.gw_out, ...), custom_call_target="tpu_custom_call" | custom-call | tf_op jit(solution)/shard_map/scatter_sums/pallas_call | solution.py:524
  154.4 5.9 %finish_weights.1 = (f32[32,80,256]{2,1,0:T(8,128)}, f32[32,80,256]{2,1,0:T(8,128)}, bf16[128,1024]{1,0:T(8,128)(2,1)}, f32[9,4096]{1,0:T(8,128)}) custom-call(bf16[32,20480]{1,0:T(8,128)(2,1)} %get-tuple-element.28.in_mine, bf16[32,20480]{1,0:T(8,128)(2,1)} %get-tuple-element.29.out_mine, bf16[128,1024]{1,0:T(8,128)(2,1)} %get-tuple-element.30.dx_mine, ...), custom_call_target="tpu_custom_call" | custom-call | tf_op jit(solution)/shard_map/finish_weights/pallas_call | solution.py:561

commit v6 on v5

--- a/solution.py
+++ b/solution.py
@@ -332,7 +332,6 @@
     weights = ((gw_in, in_mine), (gw_out, out_mine))
     enter(
         [{"rows": row} for row in group]
-        + [{"crop": 1 - y, "rows": row} for row in group]
         + [{"crop": 1 - y}]
         + [{"hid": (z + step) % depth} for step in range(1, depth)]
     )
@@ -343,6 +342,7 @@
         copy.start()
         started.append(copy)
 
+    go(kern, kern_part.at[1, 0], kern_send.at[0], kern_recv.at[1, 0], {"crop": 1 - y})
     for slot, row in enumerate((diagonal, same_chip)):
         go(dx.at[span(row, tokens), :], dx_near.at[slot], dx_send.at[slot], dx_recv.at[slot], {"rows": same_chip})
     for slot, row in enumerate(order):
@@ -369,17 +369,6 @@
     ]
     for load in dx_loads + [load for pair in gw_loads for load in pair]:
         load.start()
-    for slot, row in enumerate(group):
-        go(kern, kern_part.at[y, r], kern_send.at[slot], kern_recv.at[y, r], {"rows": row})
-        go(
-            kern,
-            kern_part.at[y, r],
-            kern_send.at[slot + 3],
-            kern_recv.at[y, r],
-            {"crop": 1 - y, "rows": row},
-        )
-    go(kern, kern_part.at[y, r], kern_send.at[6], kern_recv.at[y, r], {"crop": 1 - y})
-
     def arrived(ref, send_sem, recv_sem, target):
         remote(ref, ref, send_sem, recv_sem, target).wait_recv()
 
@@ -388,6 +377,18 @@
     dx_half[...] = (
         dx_own[0].astype(jnp.float32) + dx_near[0].astype(jnp.float32)
     ).astype(jnp.bfloat16)
+    arrived(kern_part.at[1, 0], kern_send.at[0], kern_recv.at[1, 0], {"crop": 1 - y})
+    kern_part[0, r] = (
+        kern[...].astype(jnp.float32) + kern_part[1, 0].astype(jnp.float32)
+    ).astype(jnp.bfloat16)
+    for slot, row in enumerate(group):
+        go(
+            kern_part.at[0, r],
+            kern_part.at[0, r],
+            kern_send.at[slot + 1],
+            kern_recv.at[0, r],
+            {"rows": row},
+        )
     go(dx_half, dx_far, dx_send.at[2], dx_recv.at[2], {"rows": across})
     arrived(dx_near.at[1], dx_send.at[1], dx_recv.at[1], {"rows": same_chip})
     arrived(dx_far, dx_send.at[2], dx_recv.at[2], {"rows": across})
@@ -431,16 +432,11 @@
         arrived(dx_last.at[step - 1], dx_send.at[2 + step], dx_recv.at[2 + step], {"hid": (z + step) % depth})
         total += dx_last[step - 1].astype(jnp.float32)
     dx_mine[...] = total.astype(jnp.bfloat16)
-    kern_part[y, r] = kern[...]
     for row in group:
-        for crop in (y, 1 - y):
-            arrived(kern_part.at[crop, row], kern_send.at[0], kern_recv.at[crop, row], {"rows": same_chip})
-    arrived(kern_part.at[1 - y, r], kern_send.at[0], kern_recv.at[1 - y, r], {"rows": same_chip})
+        arrived(kern_part.at[0, row], kern_send.at[0], kern_recv.at[0, row], {"rows": same_chip})
     wide = kern.shape[1]
     for row in range(4):
-        kern_all[:, row * wide : (row + 1) * wide] = kern_part[0, row].astype(
-            jnp.float32
-        ) + kern_part[1, row].astype(jnp.float32)
+        kern_all[:, row * wide : (row + 1) * wide] = kern_part[0, row].astype(jnp.float32)
     for slot, row in enumerate(order[:3]):
         for a in range(2):
             arrived(
@@ -547,7 +543,7 @@
             dma((2 + depth,)),
             dma((2, 7)),
             dma((2, 7)),
-            dma((7,)),
+            dma((4,)),
             dma((2, n_rows)),
             dma((2,)),
             dma((2, 4)),

time: 161 us -> 159 us (0.988)
  Pallas kernels: 160 us -> 158 us
    pallas_call x1, Pallas kernels: 66.7 us -> 64.6 us  [split_hidden(): pl.pallas_call(functools.partial(scatter_kernel, depth), name='scatter_su...]
where the time goes in v6:
time: 159 us; the launch traced here: 158 us
  Pallas kernels  158 us (99%)
    pallas_call x1, Pallas kernels, split_hidden(): pl.pallas_call(functools.partial(gather_kernel, depth), name='gather_part...  66.2 us
    pallas_call x1, Pallas kernels, split_hidden(): pl.pallas_call(functools.partial(scatter_kernel, depth), name='scatter_su...  64.6 us
    pallas_call x1, Pallas kernels, split_hidden(): pl.pallas_call(functools.partial(local_kernel, width, block, cols, nnz),...  20.8 us
    pallas_call x1, Pallas kernels, split_hidden(): pl.pallas_call(functools.partial(finish_kernel, all_cols, nnz), name='fin...  5.91 us

profile of v6, /device:TPU:0, one launch (start us, length us, event | category | flops | bytes accessed | tf_op | source)
XLA Modules:
  0.0 158.2 jit_solution(17631144969017572538)
XLA Ops:
  0.6 66.2 %gather_parts.1 = (bf16[512,4096]{1,0:T(8,128)(2,1)}, bf16[512,4096]{1,0:T(8,128)(2,1)}, bf16[256,5120]{1,0:T(8,128)(2,1)}, bf16[256,5120]{1,0:T(8,128)(2,1)}) custom-call(bf16[128,1024]{1,0:T(8,128)(2,1)} %bitcast.18, bf16[128,1024]{1,0:T(8,128)(2,1)} %bitcast.19, bf16[64,80,256]{2,1,0:T(8,128)(2,1)} %bitcast.16, bf16[64,80,256]{2,1,0:T(8,128)(2,1)} %bitcast.17), custom_call_target="tpu_custom_call" | custom-call | tf_op jit(solution)/shard_map/gather_parts/pallas_call | solution.py:478
  66.8 20.8 %local_math.1 = (bf16[512,4096]{1,0:T(8,128)(2,1)}, bf16[256,5120]{1,0:T(8,128)(2,1)}, bf16[256,5120]{1,0:T(8,128)(2,1)}, bf16[16,1024]{1,0:T(8,128)(2,1)}) custom-call(s32[5,16]{1,0:T(8,128)} %bitcast.20, bf16[512,4096]{1,0:T(8,128)(2,1)} %get-tuple-element.20.tok, bf16[512,4096]{1,0:T(8,128)(2,1)} %get-tuple-element.21.cot, ...), custom_call_target="tpu_custom_call" | custom-call | tf_op jit(solution)/shard_map/local_math/pallas_call | solution.py:503
  87.7 64.6 %scatter_sums.1 = (bf16[128,1024]{1,0:T(8,128)(2,1)}, bf16[32,20480]{1,0:T(8,128)(2,1)}, bf16[32,20480]{1,0:T(8,128)(2,1)}, f32[16,4096]{1,0:T(8,128)}) custom-call(bf16[512,4096]{1,0:T(8,128)(2,1)} %get-tuple-element.24.dx, bf16[256,5120]{1,0:T(8,128)(2,1)} %get-tuple-element.25.gw_in, bf16[256,5120]{1,0:T(8,128)(2,1)} %get-tuple-element.26.gw_out, ...), custom_call_target="tpu_custom_call" | custom-call | tf_op jit(solution)/shard_map/scatter_sums/pallas_call | solution.py:520
  152.3 5.9 %finish_weights.1 = (f32[32,80,256]{2,1,0:T(8,128)}, f32[32,80,256]{2,1,0:T(8,128)}, bf16[128,1024]{1,0:T(8,128)(2,1)}, f32[9,4096]{1,0:T(8,128)}) custom-call(bf16[32,20480]{1,0:T(8,128)(2,1)} %get-tuple-element.28.in_mine, bf16[32,20480]{1,0:T(8,128)(2,1)} %get-tuple-element.29.out_mine, bf16[128,1024]{1,0:T(8,128)(2,1)} %get-tuple-element.30.dx_mine, ...), custom_call_target="tpu_custom_call" | custom-call | tf_op jit(solution)/shard_map/finish_weights/pallas_call | solution.py:557
